TPU v7x, 32 devices: a whole 2x2x4 slice. The times are simulated.
32 devices in a mesh: flow: 4 (over z), cross: 8 (over y, x, core).
Axes of the slice: x: 2, y: 2, z: 4, core: 2. Of those that a mesh axis runs over, the one named last changes fastest.
Arguments:
- rhs: bfloat16 [4, 8, 16, 32, 1024], P('flow', 'cross'), may hold values from -6 to 6
- inverses: bfloat16 [4, 8, 16, 16, 1024], P('flow', 'cross'), as said below
- flux_weights: float32 [4, 8, 4, 1024], P('flow', 'cross'), may hold values from 0.05 to 0.4
- upwind_index: int32 [4, 8, 4, 1024], P('flow', 'cross'), may hold values from 0 to 1279, as said below
- sweep_order: int32 [4, 8, 1024], P('flow', 'cross'), may hold values from 0 to 1023, each once within a row
- level_counts: int32 [4, 8, 8], P('flow', 'cross'), may hold values from 32 to 128, as said below
- boundary_traces: float32 [4, 16, 3, 32, 128], P('flow', 'cross'), may hold values from -6 to 6
- trace_map: float32 [3, 16], replicated, may hold values from -0.42 to 0.42
- lift_map: float32 [16, 3], replicated, may hold values from -1.4 to 1.4
Outputs:
- solution: float32 [4, 8, 16, 32, 1024], P('flow', 'cross')
Inputs may be any that keep to these rules, and one draw needn't show every extreme that they name: `upwind_index`: an entry of a slot of level l is below 384 + l * 128: it names an inflow trace, a cross-stream rim trace or an own slot of an earlier level. Face 1 of every slot and face 0 of every slot of level 0 name inflow traces. `level_counts`: level 0 of every partition is full. `inverses`: each entry is a cell block's inverse, with unit-order diagonal.
All inputs are finite; a program needn't handle non-finite values.
Results may differ from a plain program's by a relative error of at most 0.0003.
Values sent between devices are 32-bit elements; how exact they have to be, the bound alone decides.
No kernel may reach another device: no remote copies, remote signals or barrier semaphores. Data moves between devices by JAX's collectives and lax.ppermute only.
A program may use at most 64 MiB of HBM per device.

v0:
```python
import jax
import jax.numpy as jnp
from jax import lax
from jax.sharding import PartitionSpec as P


def with_halo(cells, sides, width):
    for axis, dim in sides:
        count = lax.axis_size(axis)
        ends = count - 1
        head = lax.slice_in_dim(cells, 0, width, axis=dim)
        tail = lax.slice_in_dim(cells, cells.shape[dim] - width, cells.shape[dim], axis=dim)
        cells = jnp.concatenate(
            [
                lax.ppermute(tail, axis, [(i, (i + 1) % count) for i in range(ends)]),
                cells,
                lax.ppermute(head, axis, [((i + 1) % count, i) for i in range(ends)]),
            ],
            axis=dim,
        )
    return cells


def shifted(block, axis, distance):
    devices = range(lax.axis_size(axis))
    route = [(i - distance, i) for i in devices if i - distance in devices]
    return lax.ppermute(block, axis, route)


def sweep_group(
    level_rhs,
    level_inv,
    weights_part,
    index_part,
    counts_part,
    inflow,
    rim_pool,
    trace_map,
    lift_map,
):
    face_dofs, group_width, level_cells = inflow.shape
    cell_slots = level_rhs.shape[2]
    block_size = level_rhs.shape[0]
    level_total = cell_slots // level_cells
    own_start = level_cells + rim_pool.shape[2]
    source_pool = jnp.concatenate(
        [inflow, rim_pool, jnp.zeros((face_dofs, group_width, cell_slots), jnp.float32)], axis=2
    )
    slot_ids = jnp.arange(level_cells, dtype=jnp.int32)
    solved_levels = []
    traces = inflow
    for sweep_level in range(level_total):
        offset = sweep_level * level_cells
        faces_at = index_part[:, offset : offset + level_cells]
        weights_at = weights_part[:, offset : offset + level_cells]
        upwind_vals = source_pool[:, :, faces_at]
        carried = jnp.sum(upwind_vals * weights_at[None, None], axis=2)
        lifted = jnp.einsum("af,ftc->atc", lift_map, carried, precision=lax.Precision.HIGHEST)
        totals = level_rhs[:, :, offset : offset + level_cells] + lifted
        block_inv = level_inv[:, :, offset : offset + level_cells]
        solved = block_inv[:, 0, None, :] * totals[0][None]
        for column_pos in range(1, block_size):
            solved = solved + block_inv[:, column_pos, None, :] * totals[column_pos][None]
        alive_mask = (slot_ids < counts_part[sweep_level]).astype(jnp.float32)
        solved = solved * alive_mask
        traces = jnp.einsum("fa,atc->ftc", trace_map, solved, precision=lax.Precision.HIGHEST)
        source_pool = lax.dynamic_update_slice(source_pool, traces, (0, 0, own_start + offset))
        solved_levels.append(solved)
    return (jnp.concatenate(solved_levels, axis=2), traces)


def shards(
    rhs,
    inverses,
    flux_weights,
    upwind_index,
    sweep_order,
    level_counts,
    boundary_traces,
    trace_map,
    lift_map,
):
    slot_cells = sweep_order[0, 0]
    level_rhs = rhs[0, 0][:, :, slot_cells].astype(jnp.float32)
    level_inv = inverses[0, 0][:, :, slot_cells].astype(jnp.float32)
    weights_part = flux_weights[0, 0]
    index_part = upwind_index[0, 0]
    counts_part = level_counts[0, 0]
    extended = with_halo(boundary_traces, (("cross", 1),), 1)
    rim_pool = jnp.concatenate([extended[0, 0], extended[0, 3]], axis=2)
    block_size, tracer_total, cell_slots = level_rhs.shape
    face_dofs = trace_map.shape[0]
    level_cells = cell_slots // level_counts.shape[2]
    group_total = 1
    group_width = tracer_total // group_total
    chain_length = lax.axis_size("flow")
    position = lax.axis_index("flow")

    def run_group(group_now, inflow):
        return sweep_group(
            level_rhs,
            level_inv,
            weights_part,
            index_part,
            counts_part,
            inflow,
            rim_pool,
            trace_map,
            lift_map,
        )

    def skip_group(group_now, inflow):
        return (
            jnp.zeros((block_size, group_width, cell_slots), jnp.float32),
            jnp.zeros((face_dofs, group_width, level_cells), jnp.float32),
        )

    def take_turn(moment, carry):
        inflow, level_solution = carry
        group_now = moment - position
        active = jnp.logical_and(group_now >= 0, group_now < group_total)
        group_safe = jnp.clip(group_now, 0, group_total - 1)
        solved_group, outflow = lax.cond(active, run_group, skip_group, group_safe, inflow)
        updated = lax.dynamic_update_slice(
            level_solution, solved_group, (0, group_safe * group_width, 0)
        )
        level_solution = jnp.where(active, updated, level_solution)
        inflow = shifted(outflow, "flow", 1)
        return (inflow, level_solution)

    start_inflow = jnp.zeros((face_dofs, group_width, level_cells), jnp.float32)
    start_solution = jnp.zeros((block_size, tracer_total, cell_slots), jnp.float32)
    final_inflow, level_solution = lax.fori_loop(
        0, chain_length + group_total - 1, take_turn, (start_inflow, start_solution)
    )
    stored = (
        jnp.zeros((block_size, tracer_total, cell_slots), jnp.float32)
        .at[:, :, slot_cells]
        .set(level_solution)
    )
    return stored[None, None]


def solution(mesh):
    placed = (
        P("flow", "cross", None, None, None),
        P("flow", "cross", None, None, None),
        P("flow", "cross", None, None),
        P("flow", "cross", None, None),
        P("flow", "cross", None),
        P("flow", "cross", None),
        P("flow", "cross", None, None, None),
        P(),
        P(),
    )
    return jax.shard_map(
        shards,
        mesh=mesh,
        in_specs=placed,
        out_specs=P("flow", "cross", None, None, None),
        check_vma=False,
    )
```

profile of v0, /device:TPU:26, one launch (start us, length us, event | category | flops | bytes accessed | tf_op | source)
XLA Modules:
  0.0 667.3 jit_solution(1086123992554284342)
XLA Ops:
  0.8 1.9 collective-permute-start.2
  2.7 2.4 collective-permute-start.1
  5.9 5.8 copy.65
  11.7 10.6 %gather_fusion.9 = bf16[1024,16,32]{2,1,0:T(8,128)(2,1)} fusion(bf16[16,32,1024]{1,0,2:T(8,128)(2,1)} %bitcast.541, s32[1024]{0:T(1024)S(1)} %broadcast_clamp_fusion), kind=kCustom, calls=%fused_computation.9 | custom fusion | bytes 2101248 | tf_op jit(solution)/shard_map/gather | solution.py:84
  22.3 6.3 convert_bitcast_fusion
  28.6 4.7 copy.64
  33.3 10.5 %gather_fusion.8 = bf16[1024,16,16]{2,1,0:T(8,128)(2,1)} fusion(bf16[16,16,1024]{1,0,2:T(8,128)(2,1)} %bitcast.542, s32[1024]{0:T(1024)S(1)} %broadcast_clamp_fusion), kind=kCustom, calls=%fused_computation.8 | custom fusion | bytes 1052672 | tf_op jit(solution)/shard_map/gather | solution.py:85
  43.8 6.2 convert_bitcast_fusion.1
  50.0 6.6 copy.67
  56.6 6.2 copy.66
  62.9 468.7 %while.16 = (s32[]{:T(128)}, f32[3,32,128]{2,0,1:T(4,128)S(1)}, f32[16,32,1024]{2,0,1:T(8,128)}, s32[]{:T(128)}, f32[16,16,1024]{2,0,1:T(8,128)}, /*index=5*/f32...) while((s32[]{:T(128)}, f32[3,32,128]{2,0,1:T(4,128)S(1)}, ...), condition=%wide.region_11.12_spmd.clone, body=%wide.region_0.11_spmd.clone.sunk | while | flops 73992200 | bytes 50641576 | solution.py:133
  63.1 2.3 conditional.3
  63.7 1.6 broadcast.72
  66.7 2.0 select_select_fusion.2
  68.6 3.1 collective-permute-done
  71.7 2.2 conditional.3
  72.3 1.6 broadcast.72
  75.3 3.5 select_select_fusion.2
  78.8 2.1 collective-permute-done
  80.9 2.2 conditional.3
  81.5 1.6 broadcast.72
  84.4 3.5 select_select_fusion.2
  88.0 325.3 %collective-permute-done = f32[3,32,128]{2,0,1:T(4,128)S(1)} collective-permute-done((f32[3,32,128]{2,0,1:T(4,128)}, f32[3,32,128]{2,0,1:T(4,128)S(1)}, u32[]{:S(2)}, u32[]{:S(2)}) %collective-permute-start) | collective-permute-done | bytes 49184 | tf_op jit(solution)/shard_map/while/body/eval_jaxpr/ppermute | solution.py:27
  413.2 111.9 %conditional.3 = (f32[16,32,1024]{2,0,1:T(8,128)}, f32[3,32,128]{2,0,1:T(4,128)}) conditional(s32[]{:T(128)} %convert_element_type.85, () %tuple.315, (f32[16,16,1024]{2,0,1:T(8,128)}, f32[16,32,1024]{2,0,1:T(8,128)}, f32[3,32,128]{2,0,1:T(4,128)S(1)}, f32[3,32,128]{2,1,0:T(8,128)}, f32[3,32,128]{2,1,0:T(8,128)}, /*index=5*/s32[4,1024]{1,0:T(4,128)S(1)}, ...), branch_computations={%region_1.1_spmd, %region_2.10_spmd} | conditional | flops 72943616 | bytes 44022060 | solution.py:123
  427.3 1.6 slice_bitcast_fusion.47
  437.8 1.8 copy.38
  439.7 2.9 gather_fusion
  447.9 2.7 gather_fusion.1
  457.2 2.7 gather_fusion.2
  466.2 2.7 gather_fusion.3
  475.3 2.6 gather_fusion.4
  483.6 2.6 gather_fusion.5
  491.4 2.7 gather_fusion.6
  499.9 2.7 gather_fusion.7
  507.1 2.1 convolution_bitcast_fusion.8
  509.1 2.0 constant_dynamic-update-slice_fusion.7
  511.1 2.0 constant_dynamic-update-slice_fusion.6
  513.1 2.0 constant_dynamic-update-slice_fusion.5
  515.3 2.0 constant_dynamic-update-slice_fusion.4
  517.4 2.0 constant_dynamic-update-slice_fusion.3
  519.5 2.0 constant_dynamic-update-slice_fusion.2
  521.4 1.9 constant_dynamic-update-slice_fusion.1
  523.3 1.9 constant_dynamic-update-slice_fusion
  526.5 4.2 select_select_fusion.2
  531.5 7.7 %copy.68 = f32[1024,16,32]{2,1,0:T(8,128)} copy(f32[1024,16,32]{0,1,2:T(8,128)} %bitcast.523) | data formatting | bytes 4194304 | tf_op jit(solution)/shard_map/while | solution.py:133
  539.3 3.9 broadcast.81
  543.2 117.8 %scatter_fusion = f32[16,32,1024]{1,0,2:T(8,128)} fusion(f32[16,32,1024]{1,0,2:T(8,128)} %broadcast.81, s32[1024]{0:T(1024)S(1)} %bitcast.805, f32[1024,16,32]{2,1,0:T(8,128)} %copy.68), kind=kCustom, calls=%fused_computation.10 | custom fusion | bytes 6295552 | tf_op jit(solution)/shard_map/scatter | solution.py:139
  661.0 6.3 copy.69
  (465 shorter events, 75.7 us)
Async XLA Ops:
  0.8 62.0 %collective-permute-start.2 = (f32[1,1,3,32,128]{4,3,2,1,0:T(8,128)S(1)}, f32[1,1,3,32,128]{4,3,2,1,0:T(8,128)}, u32[]{:S(2)}, u32[]{:S(2)}) collective-permute-start(f32[1,1,3,32,128]{4,3,2,1,0:T(8,128)S(1)} %get-tuple-element.656), channel_id=1, source_target_pairs={{1,0},{2,1},{3,2},{4,3},{5,4},{6,5},{7,6},{9,8},{10,9},{11,10},{12... | collective-permute-start | bytes 147464 | tf_op jit(solution)/shard_map/ppermute | solution.py:17
  2.7 60.1 %collective-permute-start.1 = (f32[1,1,3,32,128]{4,3,2,1,0:T(8,128)S(1)}, f32[1,1,3,32,128]{4,3,2,1,0:T(8,128)}, u32[]{:S(2)}, u32[]{:S(2)}) collective-permute-start(f32[1,1,3,32,128]{4,3,2,1,0:T(8,128)S(1)} %get-tuple-element.657), channel_id=1, source_target_pairs={{0,1},{1,2},{2,3},{3,4},{4,5},{5,6},{6,7},{8,9},{9,10},{10,11},{11... | collective-permute-start | bytes 147464 | tf_op jit(solution)/shard_map/ppermute | solution.py:15
  5.9 16.4 %copy-start.173 = (s32[1024,1]{0,1:T(1,128)}, s32[1024,1]{0,1:T(1,128)S(1)}, u32[]{:S(2)}) copy-start(s32[1024,1]{0,1:T(1,128)S(1)} %compare_select_fusion.8) | copy-start | bytes 12292
  65.3 6.4 collective-permute-start
  73.9 6.9 %collective-permute-start = (f32[3,32,128]{2,0,1:T(4,128)}, f32[3,32,128]{2,0,1:T(4,128)S(1)}, u32[]{:S(2)}, u32[]{:S(2)}) collective-permute-start(f32[3,32,128]{2,0,1:T(4,128)} %get-tuple-element.739), channel_id=1, source_target_pairs={{0,8},{8,16},{16,24},{1,9},{9,17},{17,25},{2,10},{10,18},{18,26},{... | collective-permute-start | bytes 147464 | tf_op jit(solution)/shard_map/while/body/eval_jaxpr/ppermute | solution.py:27
  83.1 330.1 %collective-permute-start = (f32[3,32,128]{2,0,1:T(4,128)}, f32[3,32,128]{2,0,1:T(4,128)S(1)}, u32[]{:S(2)}, u32[]{:S(2)}) collective-permute-start(f32[3,32,128]{2,0,1:T(4,128)} %get-tuple-element.739), channel_id=1, source_target_pairs={{0,8},{8,16},{16,24},{1,9},{9,17},{17,25},{2,10},{10,18},{18,26},{... | collective-permute-start | bytes 147464 | tf_op jit(solution)/shard_map/while/body/eval_jaxpr/ppermute | solution.py:27
  84.4 328.8 %copy-start.166 = (s32[1,1,4,1024]{3,2,1,0:T(4,128)S(1)}, s32[1,1,4,1024]{3,2,1,0:T(4,128)}, u32[]{:S(2)}) copy-start(s32[1,1,4,1024]{3,2,1,0:T(4,128)} %get-tuple-element.806) | copy-start | bytes 49156 | tf_op jit(solution)/shard_map/while
  84.4 328.8 %copy-start.168 = (f32[1,1,4,1024]{3,2,1,0:T(4,128)S(1)}, f32[1,1,4,1024]{3,2,1,0:T(4,128)}, u32[]{:S(2)}) copy-start(f32[1,1,4,1024]{3,2,1,0:T(4,128)} %get-tuple-element.823) | copy-start | bytes 49156 | tf_op jit(solution)/shard_map/while
  427.2 19.4 %copy-start.133 = (f32[16,128]{1,0:T(8,128)}, f32[16,128]{1,0:T(8,128)S(1)}, u32[]{:S(2)}) copy-start(f32[16,128]{1,0:T(8,128)S(1)} %get-tuple-element.482) | copy-start | bytes 24580 | tf_op jit(solution)/shard_map/while/body/eval_jaxpr/cond
  427.2 19.4 %copy-start.134 = (f32[16,128]{1,0:T(8,128)}, f32[16,128]{1,0:T(8,128)S(1)}, u32[]{:S(2)}) copy-start(f32[16,128]{1,0:T(8,128)S(1)} %get-tuple-element.483) | copy-start | bytes 24580 | tf_op jit(solution)/shard_map/while/body/eval_jaxpr/cond
  427.2 19.4 %copy-start.135 = (f32[16,128]{1,0:T(8,128)}, f32[16,128]{1,0:T(8,128)S(1)}, u32[]{:S(2)}) copy-start(f32[16,128]{1,0:T(8,128)S(1)} %get-tuple-element.484) | copy-start | bytes 24580 | tf_op jit(solution)/shard_map/while/body/eval_jaxpr/cond
  427.2 19.4 %copy-start.136 = (f32[16,128]{1,0:T(8,128)}, f32[16,128]{1,0:T(8,128)S(1)}, u32[]{:S(2)}) copy-start(f32[16,128]{1,0:T(8,128)S(1)} %get-tuple-element.485) | copy-start | bytes 24580 | tf_op jit(solution)/shard_map/while/body/eval_jaxpr/cond
  427.2 19.4 %copy-start.137 = (f32[16,128]{1,0:T(8,128)}, f32[16,128]{1,0:T(8,128)S(1)}, u32[]{:S(2)}) copy-start(f32[16,128]{1,0:T(8,128)S(1)} %get-tuple-element.486) | copy-start | bytes 24580 | tf_op jit(solution)/shard_map/while/body/eval_jaxpr/cond
  427.2 19.4 %copy-start.138 = (f32[16,128]{1,0:T(8,128)}, f32[16,128]{1,0:T(8,128)S(1)}, u32[]{:S(2)}) copy-start(f32[16,128]{1,0:T(8,128)S(1)} %get-tuple-element.487) | copy-start | bytes 24580 | tf_op jit(solution)/shard_map/while/body/eval_jaxpr/cond
  427.2 19.4 %copy-start.139 = (f32[16,128]{1,0:T(8,128)}, f32[16,128]{1,0:T(8,128)S(1)}, u32[]{:S(2)}) copy-start(f32[16,128]{1,0:T(8,128)S(1)} %get-tuple-element.488) | copy-start | bytes 24580 | tf_op jit(solution)/shard_map/while/body/eval_jaxpr/cond
  427.3 19.4 %copy-start.140 = (f32[16,128]{1,0:T(8,128)}, f32[16,128]{1,0:T(8,128)S(1)}, u32[]{:S(2)}) copy-start(f32[16,128]{1,0:T(8,128)S(1)} %get-tuple-element.489) | copy-start | bytes 24580 | tf_op jit(solution)/shard_map/while/body/eval_jaxpr/cond
  427.3 19.4 %copy-start.141 = (f32[16,128]{1,0:T(8,128)}, f32[16,128]{1,0:T(8,128)S(1)}, u32[]{:S(2)}) copy-start(f32[16,128]{1,0:T(8,128)S(1)} %get-tuple-element.490) | copy-start | bytes 24580 | tf_op jit(solution)/shard_map/while/body/eval_jaxpr/cond
  427.3 19.4 %copy-start.142 = (f32[16,128]{1,0:T(8,128)}, f32[16,128]{1,0:T(8,128)S(1)}, u32[]{:S(2)}) copy-start(f32[16,128]{1,0:T(8,128)S(1)} %get-tuple-element.491) | copy-start | bytes 24580 | tf_op jit(solution)/shard_map/while/body/eval_jaxpr/cond
  427.3 19.4 %copy-start.143 = (f32[16,128]{1,0:T(8,128)}, f32[16,128]{1,0:T(8,128)S(1)}, u32[]{:S(2)}) copy-start(f32[16,128]{1,0:T(8,128)S(1)} %get-tuple-element.492) | copy-start | bytes 24580 | tf_op jit(solution)/shard_map/while/body/eval_jaxpr/cond
  427.3 19.4 %copy-start.144 = (f32[16,128]{1,0:T(8,128)}, f32[16,128]{1,0:T(8,128)S(1)}, u32[]{:S(2)}) copy-start(f32[16,128]{1,0:T(8,128)S(1)} %get-tuple-element.493) | copy-start | bytes 24580 | tf_op jit(solution)/shard_map/while/body/eval_jaxpr/cond
  427.3 19.4 %copy-start.145 = (f32[16,128]{1,0:T(8,128)}, f32[16,128]{1,0:T(8,128)S(1)}, u32[]{:S(2)}) copy-start(f32[16,128]{1,0:T(8,128)S(1)} %get-tuple-element.494) | copy-start | bytes 24580 | tf_op jit(solution)/shard_map/while/body/eval_jaxpr/cond
  427.3 19.4 %copy-start.146 = (f32[16,128]{1,0:T(8,128)}, f32[16,128]{1,0:T(8,128)S(1)}, u32[]{:S(2)}) copy-start(f32[16,128]{1,0:T(8,128)S(1)} %get-tuple-element.495) | copy-start | bytes 24580 | tf_op jit(solution)/shard_map/while/body/eval_jaxpr/cond
  505.1 12.2 %copy-start.26 = (f32[1,32,128]{2,0,1:T(1,128)S(1)}, f32[1,32,128]{2,0,1:T(1,128)}, u32[]{:S(2)}) copy-start(f32[1,32,128]{2,0,1:T(1,128)} %copy-done.25) | copy-start | bytes 49156 | tf_op jit(solution)/shard_map/while/body/eval_jaxpr/cond
  505.1 12.2 %copy-start.28 = (f32[1,32,128]{2,0,1:T(1,128)S(1)}, f32[1,32,128]{2,0,1:T(1,128)}, u32[]{:S(2)}) copy-start(f32[1,32,128]{2,0,1:T(1,128)} %copy-done.27) | copy-start | bytes 49156 | tf_op jit(solution)/shard_map/while/body/eval_jaxpr/cond
  505.1 12.2 %copy-start.30 = (f32[1,32,128]{2,0,1:T(1,128)S(1)}, f32[1,32,128]{2,0,1:T(1,128)}, u32[]{:S(2)}) copy-start(f32[1,32,128]{2,0,1:T(1,128)} %copy-done.29) | copy-start | bytes 49156 | tf_op jit(solution)/shard_map/while/body/eval_jaxpr/cond
  505.1 12.2 %copy-start.32 = (f32[1,32,128]{2,0,1:T(1,128)S(1)}, f32[1,32,128]{2,0,1:T(1,128)}, u32[]{:S(2)}) copy-start(f32[1,32,128]{2,0,1:T(1,128)} %copy-done.31) | copy-start | bytes 49156 | tf_op jit(solution)/shard_map/while/body/eval_jaxpr/cond
  505.1 12.2 %copy-start.34 = (f32[1,32,128]{2,0,1:T(1,128)S(1)}, f32[1,32,128]{2,0,1:T(1,128)}, u32[]{:S(2)}) copy-start(f32[1,32,128]{2,0,1:T(1,128)} %copy-done.33) | copy-start | bytes 49156 | tf_op jit(solution)/shard_map/while/body/eval_jaxpr/cond
  505.1 12.2 %copy-start.36 = (f32[1,32,128]{2,0,1:T(1,128)S(1)}, f32[1,32,128]{2,0,1:T(1,128)}, u32[]{:S(2)}) copy-start(f32[1,32,128]{2,0,1:T(1,128)} %copy-done.35) | copy-start | bytes 49156 | tf_op jit(solution)/shard_map/while/body/eval_jaxpr/cond
  505.1 12.2 %copy-start.38 = (f32[1,32,128]{2,0,1:T(1,128)S(1)}, f32[1,32,128]{2,0,1:T(1,128)}, u32[]{:S(2)}) copy-start(f32[1,32,128]{2,0,1:T(1,128)} %copy-done.37) | copy-start | bytes 49156 | tf_op jit(solution)/shard_map/while/body/eval_jaxpr/cond
  505.1 12.2 %copy-start.40 = (f32[1,32,128]{2,0,1:T(1,128)S(1)}, f32[1,32,128]{2,0,1:T(1,128)}, u32[]{:S(2)}) copy-start(f32[1,32,128]{2,0,1:T(1,128)} %copy-done.39) | copy-start | bytes 49156 | tf_op jit(solution)/shard_map/while/body/eval_jaxpr/cond
  505.2 12.2 %copy-start.42 = (f32[1,32,128]{2,0,1:T(1,128)S(1)}, f32[1,32,128]{2,0,1:T(1,128)}, u32[]{:S(2)}) copy-start(f32[1,32,128]{2,0,1:T(1,128)} %copy-done.41) | copy-start | bytes 49156 | tf_op jit(solution)/shard_map/while/body/eval_jaxpr/cond
  505.2 12.2 %copy-start.44 = (f32[1,32,128]{2,0,1:T(1,128)S(1)}, f32[1,32,128]{2,0,1:T(1,128)}, u32[]{:S(2)}) copy-start(f32[1,32,128]{2,0,1:T(1,128)} %copy-done.43) | copy-start | bytes 49156 | tf_op jit(solution)/shard_map/while/body/eval_jaxpr/cond
  505.2 12.2 %copy-start.46 = (f32[1,32,128]{2,0,1:T(1,128)S(1)}, f32[1,32,128]{2,0,1:T(1,128)}, u32[]{:S(2)}) copy-start(f32[1,32,128]{2,0,1:T(1,128)} %copy-done.45) | copy-start | bytes 49156 | tf_op jit(solution)/shard_map/while/body/eval_jaxpr/cond
  505.2 12.2 %copy-start.48 = (f32[1,32,128]{2,0,1:T(1,128)S(1)}, f32[1,32,128]{2,0,1:T(1,128)}, u32[]{:S(2)}) copy-start(f32[1,32,128]{2,0,1:T(1,128)} %copy-done.47) | copy-start | bytes 49156 | tf_op jit(solution)/shard_map/while/body/eval_jaxpr/cond
  505.2 12.2 %copy-start.50 = (f32[1,32,128]{2,0,1:T(1,128)S(1)}, f32[1,32,128]{2,0,1:T(1,128)}, u32[]{:S(2)}) copy-start(f32[1,32,128]{2,0,1:T(1,128)} %copy-done.49) | copy-start | bytes 49156 | tf_op jit(solution)/shard_map/while/body/eval_jaxpr/cond
  506.7 12.7 %copy-start.2 = (f32[1,32,128]{2,0,1:T(1,128)S(1)}, f32[1,32,128]{2,0,1:T(1,128)}, u32[]{:S(2)}) copy-start(f32[1,32,128]{2,0,1:T(1,128)} %copy-done.1) | copy-start | bytes 49156 | tf_op jit(solution)/shard_map/while/body/eval_jaxpr/cond
  506.7 12.7 %copy-start.4 = (f32[1,32,128]{2,0,1:T(1,128)S(1)}, f32[1,32,128]{2,0,1:T(1,128)}, u32[]{:S(2)}) copy-start(f32[1,32,128]{2,0,1:T(1,128)} %copy-done.3) | copy-start | bytes 49156 | tf_op jit(solution)/shard_map/while/body/eval_jaxpr/cond
  506.7 12.7 %copy-start.6 = (f32[1,32,128]{2,0,1:T(1,128)S(1)}, f32[1,32,128]{2,0,1:T(1,128)}, u32[]{:S(2)}) copy-start(f32[1,32,128]{2,0,1:T(1,128)} %copy-done.5) | copy-start | bytes 49156 | tf_op jit(solution)/shard_map/while/body/eval_jaxpr/cond
  506.7 12.7 %copy-start.8 = (f32[1,32,128]{2,0,1:T(1,128)S(1)}, f32[1,32,128]{2,0,1:T(1,128)}, u32[]{:S(2)}) copy-start(f32[1,32,128]{2,0,1:T(1,128)} %copy-done.7) | copy-start | bytes 49156 | tf_op jit(solution)/shard_map/while/body/eval_jaxpr/cond
  506.7 12.7 %copy-start.10 = (f32[1,32,128]{2,0,1:T(1,128)S(1)}, f32[1,32,128]{2,0,1:T(1,128)}, u32[]{:S(2)}) copy-start(f32[1,32,128]{2,0,1:T(1,128)} %copy-done.9) | copy-start | bytes 49156 | tf_op jit(solution)/shard_map/while/body/eval_jaxpr/cond
  506.7 12.7 %copy-start.12 = (f32[1,32,128]{2,0,1:T(1,128)S(1)}, f32[1,32,128]{2,0,1:T(1,128)}, u32[]{:S(2)}) copy-start(f32[1,32,128]{2,0,1:T(1,128)} %copy-done.11) | copy-start | bytes 49156 | tf_op jit(solution)/shard_map/while/body/eval_jaxpr/cond
  506.8 12.7 %copy-start.14 = (f32[1,32,128]{2,0,1:T(1,128)S(1)}, f32[1,32,128]{2,0,1:T(1,128)}, u32[]{:S(2)}) copy-start(f32[1,32,128]{2,0,1:T(1,128)} %copy-done.13) | copy-start | bytes 49156 | tf_op jit(solution)/shard_map/while/body/eval_jaxpr/cond
  506.8 12.7 %copy-start.16 = (f32[1,32,128]{2,0,1:T(1,128)S(1)}, f32[1,32,128]{2,0,1:T(1,128)}, u32[]{:S(2)}) copy-start(f32[1,32,128]{2,0,1:T(1,128)} %copy-done.15) | copy-start | bytes 49156 | tf_op jit(solution)/shard_map/while/body/eval_jaxpr/cond
  506.8 12.7 %copy-start.18 = (f32[1,32,128]{2,0,1:T(1,128)S(1)}, f32[1,32,128]{2,0,1:T(1,128)}, u32[]{:S(2)}) copy-start(f32[1,32,128]{2,0,1:T(1,128)} %copy-done.17) | copy-start | bytes 49156 | tf_op jit(solution)/shard_map/while/body/eval_jaxpr/cond
  506.8 12.7 %copy-start.20 = (f32[1,32,128]{2,0,1:T(1,128)S(1)}, f32[1,32,128]{2,0,1:T(1,128)}, u32[]{:S(2)}) copy-start(f32[1,32,128]{2,0,1:T(1,128)} %copy-done.19) | copy-start | bytes 49156 | tf_op jit(solution)/shard_map/while/body/eval_jaxpr/cond
  506.8 12.7 %copy-start.22 = (f32[1,32,128]{2,0,1:T(1,128)S(1)}, f32[1,32,128]{2,0,1:T(1,128)}, u32[]{:S(2)}) copy-start(f32[1,32,128]{2,0,1:T(1,128)} %copy-done.21) | copy-start | bytes 49156 | tf_op jit(solution)/shard_map/while/body/eval_jaxpr/cond
  506.8 12.7 %copy-start.24 = (f32[1,32,128]{2,0,1:T(1,128)S(1)}, f32[1,32,128]{2,0,1:T(1,128)}, u32[]{:S(2)}) copy-start(f32[1,32,128]{2,0,1:T(1,128)} %copy-done.23) | copy-start | bytes 49156 | tf_op jit(solution)/shard_map/while/body/eval_jaxpr/cond
  525.2 6.4 collective-permute-start
  (144 other events, 921.2 us)
where the time goes:
time: 673 us; the launch traced here: 667 us
  waiting for transfers between devices  331 us (49%)
  local copies, waits for them, and re-layouts  241 us (36%)
  other arithmetic  59.8 us (9%)
  matrix products  22.4 us (3%)
  starting transfers between devices  9.44 us (1%)
    ppermute x4, waiting for transfers between devices, shifted(): return lax.ppermute(block, axis, route)  331 us
    scatter x1, local copies, waits for them, and re-layouts, shards(): stored = jnp.zeros((block_size, tracer_total, cell_slots), jnp.float32).a...  118 us
    gather x16, local copies, waits for them, and re-layouts, sweep_group(): upwind_vals = source_pool[:, :, faces_at]  33.6 us
    unnamed x18, local copies, waits for them, and re-layouts  23.4 us
    cond x7, other arithmetic  13.8 us
  transfers between devices with their start and end apart: 6, of which 4 were waited for; matrix products, arithmetic and copies ran while one was open for 11% of the time, Pallas kernels for 0%

commit v1 on v0

v1 whole, which is shorter than its diff:
```python
import functools

import jax
import jax.numpy as jnp
from jax import lax
from jax.experimental import pallas as pl
from jax.experimental.pallas import tpu as pltpu
from jax.sharding import PartitionSpec as P

F32 = jnp.float32
BF16 = jnp.bfloat16
LANES = 128
SUB = 8
WROWS = 16
VM = pl.BlockSpec(memory_space=pltpu.VMEM)
HIGHEST = lax.Precision.HIGHEST


def params(mib):
    return pltpu.CompilerParams(vmem_limit_bytes=mib << 20)


def in_vmem(array):
    return pltpu.with_memory_space_constraint(array, pltpu.VMEM)


def in_hbm(array):
    return pltpu.with_memory_space_constraint(array, pltpu.HBM)


def split(values):
    high = values.astype(BF16)
    return high, (values - high.astype(F32)).astype(BF16)


def iota(shape, dim):
    return lax.broadcasted_iota(jnp.int32, shape, dim)


def coefficients(trace_map, lift_map, block):
    faces = trace_map.shape[0]
    width = block * block
    row = iota((block, width), 0)
    lane = iota((block, width), 1)
    first = lane // block == row
    second = lane % block == row
    spread_t = jnp.dot(trace_map, first.astype(F32), precision=HIGHEST)
    spread_l = jnp.dot(lift_map, second.astype(F32), precision=HIGHEST)
    rows = [jnp.where(second, spread_t[f : f + 1], 0.0) for f in range(faces)]
    rows += [jnp.where(first, spread_l[g : g + 1], 0.0) for g in range(faces)]
    rows += [spread_t[f : f + 1] * spread_l for f in range(faces)]
    rows.append(jnp.zeros((WROWS - faces * faces, width), F32))
    return jnp.concatenate(rows, axis=0)


def prepare(
    counts_hbm,
    inv_hbm,
    rhs_hbm,
    order_hbm,
    index_hbm,
    weights_hbm,
    trace_hbm,
    lift_hbm,
    r_out,
    w_out,
    il_out,
    q_out,
    inv,
    rhs,
    index,
    weights,
    live_out,
    p_out,
    counts,
    order,
    trace_map,
    lift_map,
    ti,
    stacked,
    sem,
):
    pairs = [
        (order_hbm, order),
        (trace_hbm, trace_map),
        (lift_hbm, lift_map),
        (inv_hbm, inv),
        (rhs_hbm, rhs),
        (index_hbm, index),
        (weights_hbm, weights),
        (counts_hbm, counts),
    ]
    copies = [pltpu.make_async_copy(a, b, sem.at[i]) for i, (a, b) in enumerate(pairs)]
    for copy in copies:
        copy.start()
    block, _, cells = inv.shape
    faces = trace_map.shape[0]
    tracers = rhs.shape[1]
    rows = faces * tracers
    half = rows + WROWS
    copies[0].wait()
    for j in range(cells // LANES):
        hit = iota((LANES, cells), 0) + j * LANES == order[...]
        q_out[j * LANES : (j + 1) * LANES, :] = jnp.where(hit, 1.0, 0.0).astype(BF16)
    copies[1].wait()
    copies[2].wait()
    high, low = split(coefficients(trace_map[...], lift_map[...], block))
    copies[3].wait()
    flat = inv[...].reshape(block * block, cells)
    made = jnp.dot(high, flat, preferred_element_type=F32) + jnp.dot(
        low, flat, preferred_element_type=F32
    )
    ti[...] = made[: faces * block]
    il_out[...] = made[faces * block : 2 * faces * block]
    high, low = split(made[2 * faces * block :])
    stacked[rows:half, :] = high
    stacked[half + rows :, :] = low
    copies[4].wait()
    for j in range(cells // LANES):
        at = pl.ds(j * LANES, LANES)
        sums = [None] * faces
        for b in range(block):
            source = rhs[b, :, at].astype(F32)
            for f in range(faces):
                term = ti[f * block + b : f * block + b + 1, at] * source
                sums[f] = term if sums[f] is None else sums[f] + term
        for f in range(faces):
            high, low = split(sums[f])
            stacked[f * tracers : (f + 1) * tracers, at] = high
            stacked[half + f * tracers : half + (f + 1) * tracers, at] = low
    slots = jnp.dot(stacked[...], q_out[...], preferred_element_type=F32)
    copies[7].wait()
    for level in range(cells // LANES):
        lo, hi = level * LANES, (level + 1) * LANES
        live = (iota((1, LANES), 1) < counts[level]).astype(F32)
        live_out[:, lo:hi] = live
        r_out[:, lo:hi] = (slots[:rows, lo:hi] + slots[half : half + rows, lo:hi]) * live
        w_out[:, lo:hi] = (slots[rows:half, lo:hi] + slots[half + rows :, lo:hi]) * live
    copies[5].wait()
    copies[6].wait()


def gathered(source, lane):
    return jnp.take_along_axis(source, lane, axis=1, mode="promise_in_bounds")


def face_values(faces_at, level, sources, index, count):
    at = index[faces_at : faces_at + 1, level * LANES : (level + 1) * LANES]
    at = jnp.broadcast_to(at, (SUB, LANES))
    lane = at & (LANES - 1)
    group = lax.shift_right_logical(at, LANES.bit_length() - 1)
    values = [None] * count
    for code, read in sources:
        here = group == code
        for i in range(count):
            got = gathered(read(i), lane)
            values[i] = jnp.where(here, got, 0.0 if values[i] is None else values[i])
    return values


def rows_of(i):
    return slice(i * SUB, (i + 1) * SUB)


def inflow_only(face, level):
    return face == 1 or (face == 0 and level == 0)


def rim_part(ring_a, ring_b, index, weights, e_out, rim, *, cross):
    column = lax.axis_index(cross)
    last = lax.axis_size(cross) - 1
    even = column % 2 == 0
    faces, cells = index.shape
    rows = e_out.shape[0]
    count = rows // SUB
    has_lower = column > 0
    has_upper = column < last
    lower = jnp.where(even, ring_b[1], ring_a[1])
    upper = jnp.where(even, ring_a[0], ring_b[0])
    rim[0] = jnp.where(has_lower, lower, 0.0)
    rim[1] = jnp.where(has_upper, upper, 0.0)
    for level in range(cells // LANES):
        at = slice(level * LANES, (level + 1) * LANES)
        sums = [None] * count
        for face in range(faces):
            if inflow_only(face, level):
                continue
            sources = [(1 + s, lambda i, s=s: rim[s, rows_of(i), :]) for s in range(2)]
            values = face_values(face, level, sources, index, count)
            weight = jnp.broadcast_to(weights[face : face + 1, at], (SUB, LANES))
            for i in range(count):
                term = values[i] * weight
                sums[i] = term if sums[i] is None else sums[i] + term
        for i in range(count):
            e_out[rows_of(i), at] = sums[i]


def sweep(inflow, r, w, index, weights, e_out, traces_out, pool, face_dofs):
    faces, cells = index.shape
    levels = cells // LANES
    count = e_out.shape[0] // SUB
    per_dof = count // face_dofs
    for level in range(levels):
        at = slice(level * LANES, (level + 1) * LANES)
        sums = [e_out[rows_of(i), at] for i in range(count)]
        for face in range(faces):
            sources = []
            if inflow is not None:
                sources.append((0, lambda i: inflow[rows_of(i), :]))
            if not inflow_only(face, level):
                sources += [
                    (3 + s, lambda i, s=s: pool[s, rows_of(i), :]) for s in range(level)
                ]
            if not sources:
                continue
            values = face_values(face, level, sources, index, count)
            weight = jnp.broadcast_to(weights[face : face + 1, at], (SUB, LANES))
            for i in range(count):
                sums[i] = sums[i] + values[i] * weight
        for i in range(count):
            e_out[rows_of(i), at] = sums[i]
        for f in range(face_dofs):
            mix = [
                jnp.broadcast_to(w[face_dofs * f + g : face_dofs * f + g + 1, at], (SUB, LANES))
                for g in range(face_dofs)
            ]
            for q in range(per_dof):
                i = f * per_dof + q
                value = r[rows_of(i), at]
                for g in range(face_dofs):
                    value = value + mix[g] * sums[g * per_dof + q]
                if level < levels - 1:
                    pool[level, rows_of(i), :] = value
                else:
                    traces_out[rows_of(i), :] = value


def local_group(j, live, inv, rhs, q, p_out, wide):
    block = inv.shape[0]
    cells = rhs.shape[2]
    start = pl.multiple_of(j * LANES, LANES)
    at = pl.ds(start, LANES)
    rows = jnp.broadcast_to(live[...], (WROWS, cells)).astype(BF16)
    mask = lax.dot_general(
        rows, q[at, :], (((1,), (1,)), ((), ())), preferred_element_type=F32
    )[:1]
    for a in range(block):
        wide[a * block : (a + 1) * block, :] = inv[a, :, at].astype(F32) * mask
    step = 4

    def some(part, carry):
        sums = [None] * step
        for b in range(block):
            source = rhs[b, :, at].astype(F32)
            for i in range(step):
                row = (part * step + i) * block + b
                term = wide[pl.ds(row, 1), :] * source
                sums[i] = term if sums[i] is None else sums[i] + term
        for i in range(step):
            p_out[part * step + i, :, at] = sums[i]
        return carry

    lax.fori_loop(0, block // step, some, 0)


def turn(*refs, moment, flow, face_dofs, last):
    refs = list(refs)
    inflow = refs.pop(0) if moment > 0 else None
    live, r, w, index, weights, inv, rhs, q, _, _, e_out, p_out, traces_out, pool, wide = refs
    position = lax.axis_index(flow)
    others = lax.axis_size(flow) - 1
    groups = index.shape[1] // LANES

    def some_groups(first, end):
        lax.fori_loop(
            first, end, lambda j, c: (local_group(j, live, inv, rhs, q, p_out, wide), c)[1], 0
        )

    @pl.when(position == moment)
    def _():
        sweep(inflow, r, w, index, weights, e_out, traces_out, pool, face_dofs)
        if others == 0:
            some_groups(0, groups)

    if others > 0:

        @pl.when(position != moment)
        def _():
            part = jnp.where(position < moment, moment - 1, moment)
            some_groups(part * groups // others, (part + 1) * groups // others)


def finish(live, e, p, il, q, out, stacked, done, sem):
    block, tracers, cells = p.shape
    rows = e.shape[0]
    face_dofs = rows // tracers
    high, low = split(e[...] * live[...])
    stacked[:rows, :] = high
    stacked[rows:, :] = low
    width = 2 * LANES
    copies = []
    for jj in range(cells // width):
        back = lax.dot_general(
            stacked[...],
            q[jj * width : (jj + 1) * width, :],
            (((1,), (1,)), ((), ())),
            preferred_element_type=F32,
        )
        for k in range(2):
            at = pl.ds(jj * width + k * LANES, LANES)
            part = slice(k * LANES, (k + 1) * LANES)
            carried = [
                back[g * tracers : (g + 1) * tracers, part]
                + back[rows + g * tracers : rows + (g + 1) * tracers, part]
                for g in range(face_dofs)
            ]
            for a in range(block):
                value = p[a, :, at]
                for g in range(face_dofs):
                    value = value + il[g * block + a : g * block + a + 1, at] * carried[g]
                done[a, :, at] = value
        at = pl.ds(jj * width, width)
        copy = pltpu.make_async_copy(done.at[:, :, at], out.at[:, :, at], sem.at[jj])
        copy.start()
        copies.append(copy)
    for copy in copies:
        copy.wait()


def swaps(flows, columns, partner):
    pairs = []
    for f in range(flows):
        for c in range(columns):
            to_f, to_c = partner(f, c)
            if not (0 <= to_f < flows and 0 <= to_c < columns):
                to_f, to_c = f, c
            pairs.append((f * columns + c, to_f * columns + to_c))
    return pairs


def rim_partner(first, columns):
    def partner(f, c):
        other = c + 1 if c % 2 == first else c - 1
        return (f, other) if 0 <= other < columns else (f ^ 1, c)

    return partner


def hop_partner(moment):
    def partner(f, c):
        return (2 * moment + 1 - f, c) if f in (moment, moment + 1) else (f, c ^ 1)

    return partner


def shards(
    rhs,
    inverses,
    flux_weights,
    upwind_index,
    sweep_order,
    level_counts,
    boundary_traces,
    trace_map,
    lift_map,
):
    _, _, block, tracers, cells = rhs.shape
    face_dofs = trace_map.shape[0]
    rows = face_dofs * tracers
    flows = lax.axis_size("flow")
    columns = lax.axis_size("cross")
    edges = boundary_traces.reshape(2, rows, LANES)
    axes = ("flow", "cross")
    ring_a = lax.ppermute(edges, axes, swaps(flows, columns, rim_partner(0, columns)))
    ring_b = lax.ppermute(edges, axes, swaps(flows, columns, rim_partner(1, columns)))
    faces = upwind_index.shape[2]
    far = pl.BlockSpec(memory_space=pltpu.HBM)

    r, w, il, q, inv, rhs, index, weights, live, p = pl.pallas_call(
        prepare,
        out_shape=(
            pltpu.VMEM((rows, cells), F32),
            pltpu.VMEM((WROWS, cells), F32),
            pltpu.VMEM((face_dofs * block, cells), F32),
            pltpu.VMEM((cells, cells), BF16),
            pltpu.VMEM((block, block, cells), BF16),
            pltpu.VMEM((block, tracers, cells), BF16),
            pltpu.VMEM((faces, cells), jnp.int32),
            pltpu.VMEM((faces, cells), F32),
            pltpu.VMEM((1, cells), F32),
            pltpu.VMEM((block, tracers, cells), F32),
        ),
        in_specs=[far] * 8,
        out_specs=(VM,) * 10,
        scratch_shapes=[
            pltpu.SMEM((cells // LANES,), jnp.int32),
            pltpu.VMEM((1, cells), jnp.int32),
            pltpu.VMEM((face_dofs, block), F32),
            pltpu.VMEM((face_dofs, block), F32),
            pltpu.VMEM((face_dofs * block, cells), F32),
            pltpu.VMEM((2 * (rows + WROWS), cells), BF16),
            pltpu.SemaphoreType.DMA((8,)),
        ],
        compiler_params=params(12),
        name="prepare",
    )(
        in_hbm(level_counts[0, 0]),
        in_hbm(inverses[0, 0]),
        in_hbm(rhs[0, 0]),
        in_hbm(sweep_order[0]),
        in_hbm(upwind_index[0, 0]),
        in_hbm(flux_weights[0, 0]),
        in_hbm(trace_map),
        in_hbm(lift_map.T),
    )

    e = pl.pallas_call(
        functools.partial(rim_part, cross="cross"),
        out_shape=pltpu.VMEM((rows, cells), F32),
        in_specs=[VM] * 4,
        out_specs=VM,
        scratch_shapes=[pltpu.VMEM((2, rows, LANES), F32)],
        compiler_params=params(4),
        name="rim",
    )(in_vmem(ring_a), in_vmem(ring_b), index, weights)

    received = None
    for moment in range(flows):
        last = moment == flows - 1
        given = [] if moment == 0 else [in_vmem(received)]
        n = len(given)
        given += [live, r, w, index, weights, inv, rhs, q, e, p]
        shapes = [
            pltpu.VMEM((rows, cells), F32),
            pltpu.VMEM((block, tracers, cells), F32),
        ]
        sent = pltpu.VMEM((rows, LANES), F32)
        made = pl.pallas_call(
            functools.partial(turn, moment=moment, flow="flow", face_dofs=face_dofs, last=last),
            out_shape=shapes if last else shapes + [sent],
            in_specs=[VM] * (n + 10),
            out_specs=[VM] * (2 if last else 3),
            input_output_aliases={len(given) - 2: 0, len(given) - 1: 1},
            scratch_shapes=([sent] if last else [])
            + [
                pltpu.VMEM((cells // LANES, rows, LANES), F32),
                pltpu.VMEM((block * block, LANES), F32),
            ],
            compiler_params=params(4),
            name=f"turn{moment}",
        )(*given)
        e, p = made[:2]
        if not last:
            received = lax.ppermute(
                made[2], axes, swaps(flows, columns, hop_partner(moment))
            )

    out = pl.pallas_call(
        finish,
        out_shape=jax.ShapeDtypeStruct((block, tracers, cells), F32),
        in_specs=[VM] * 5,
        out_specs=pl.BlockSpec(memory_space=pltpu.HBM),
        scratch_shapes=[
            pltpu.VMEM((2 * rows, cells), BF16),
            pltpu.VMEM((block, tracers, cells), F32),
            pltpu.SemaphoreType.DMA((cells // (2 * LANES),)),
        ],
        compiler_params=params(12),
        name="finish",
    )(live, e, p, il, q)
    return out[None, None]


def solution(mesh):
    placed = (
        P("flow", "cross", None, None, None),
        P("flow", "cross", None, None, None),
        P("flow", "cross", None, None),
        P("flow", "cross", None, None),
        P("flow", "cross", None),
        P("flow", "cross", None),
        P("flow", "cross", None, None, None),
        P(),
        P(),
    )
    return jax.shard_map(
        shards,
        mesh=mesh,
        in_specs=placed,
        out_specs=P("flow", "cross", None, None, None),
        check_vma=False,
    )
```

time: 673 us -> 26.1 us (0.04)
  the two profiles are of different devices: /device:TPU:26 before, /device:TPU:20 now
where the time goes in v1:
time: 26.1 us; the launch traced here: 26 us
  Pallas kernels  12.5 us (48%)
  waiting for transfers between devices  8.18 us (31%)
  starting transfers between devices  5.19 us (20%)
    ppermute x3, waiting for transfers between devices, shards(): lax.ppermute(made[2], axes, swaps(flows, columns, hop_partner(moment)))  7.36 us
    pallas_call x4, Pallas kernels, shards(): pl.pallas_call(functools.partial(turn, moment=moment, flow='flow', face_d...  6.42 us
    ppermute x3, starting transfers between devices, shards(): lax.ppermute(made[2], axes, swaps(flows, columns, hop_partner(moment)))  3.59 us
    pallas_call x1, Pallas kernels, shards(): pl.pallas_call(prepare, out_shape=(pltpu.VMEM((rows, cells), F32), pltpu....  2.86 us
    pallas_call x1, Pallas kernels, shards(): pl.pallas_call(finish, out_shape=jax.ShapeDtypeStruct((block, tracers, ce...  2.52 us
    ppermute x1, starting transfers between devices, shards(): lax.ppermute(edges, axes, swaps(flows, columns, rim_partner(1, columns)))  0.87 us
    ppermute x1, waiting for transfers between devices, shards(): lax.ppermute(edges, axes, swaps(flows, columns, rim_partner(1, columns)))  0.81 us
    ppermute x1, starting transfers between devices, shards(): lax.ppermute(edges, axes, swaps(flows, columns, rim_partner(0, columns)))  0.73 us
  transfers between devices with their start and end apart: 5, of which 4 were waited for; matrix products, arithmetic and copies ran while one was open for 0% of the time, Pallas kernels for 11%

profile of v1, /device:TPU:20, one launch (start us, length us, event | category | flops | bytes accessed | tf_op | source)
XLA Modules:
  0.0 26.0 jit_solution(8228763911230163842)
XLA Ops:
  0.0 0.9 %collective-permute-start.1 = (f32[2,96,128]{2,1,0:T(8,128)}, f32[2,96,128]{2,1,0:T(8,128)S(1)}, u32[]{:S(2)}, u32[]{:S(2)}) collective-permute-start(f32[2,96,128]{2,1,0:T(8,128)} %bitcast.16), channel_id=1, source_target_pairs={{0,8},{1,2},{2,1},{3,4},{4,3},{5,6},{6,5},{7,15},{8,0},{9,10},{10,... | collective-permute-start | bytes 294920 | tf_op jit(solution)/shard_map/ppermute | solution.py:375
  0.9 0.7 %collective-permute-start = (f32[2,96,128]{2,1,0:T(8,128)}, f32[2,96,128]{2,1,0:T(8,128)S(1)}, u32[]{:S(2)}, u32[]{:S(2)}) collective-permute-start(f32[2,96,128]{2,1,0:T(8,128)} %bitcast.17), channel_id=1, source_target_pairs={{0,1},{1,0},{2,3},{3,2},{4,5},{5,4},{6,7},{7,6},{8,9},{9,8},{10,11... | collective-permute-start | bytes 294920 | tf_op jit(solution)/shard_map/ppermute | solution.py:374
  1.6 2.9 %prepare.1 = (f32[96,1024]{1,0:T(8,128)S(1)}, f32[16,1024]{1,0:T(8,128)S(1)}, f32[48,1024]{1,0:T(8,128)S(1)}, bf16[1024,1024]{1,0:T(8,128)(2,1)S(1)}, bf16[16,16...) custom-call(s32[8]{0:T(128)} %bitcast.15, ...), custom_call_target="tpu_custom_call" | custom-call | tf_op jit(solution)/shard_map/prepare/pallas_call | solution.py:379
  4.5 0.8 %collective-permute-done.1.ring_b = f32[2,96,128]{2,1,0:T(8,128)S(1)} collective-permute-done((f32[2,96,128]{2,1,0:T(8,128)}, f32[2,96,128]{2,1,0:T(8,128)S(1)}, u32[]{:S(2)}, u32[]{:S(2)}) %collective-permute-start.1) | collective-permute-done | bytes 98336 | tf_op jit(solution)/shard_map/ppermute | solution.py:375
  5.3 0.0 collective-permute-done.ring_a
  5.3 0.7 %rim.1.refs_8_ = f32[96,1024]{1,0:T(8,128)S(1)} custom-call(f32[2,96,128]{2,1,0:T(8,128)S(1)} %collective-permute-done.ring_a, f32[2,96,128]{2,1,0:T(8,128)S(1)} %collective-permute-done.1.ring_b, s32[4,1024]{1,0:T(4,128)S(1)} %get-tuple-element.29.index.refs_3_.refs_4_, f32[4,1024]{1,0:T(4,128)S(1)} %get-tuple-element.30.weights.refs_4_.refs_5_), custom_call_target="tpu_custom_call" | custom-call | tf_op jit(solution)/shard_map/rim/pallas_call | solution.py:417
  6.0 1.2 %turn0.1 = (f32[96,1024]{1,0:T(8,128)S(1)}, f32[16,32,1024]{2,1,0:T(8,128)S(1)}, f32[96,128]{1,0:T(8,128)S(1)}) custom-call(f32[1,1024]{1,0:T(1,128)S(1)} %get-tuple-element.26.refs_0_.refs_1_.live, f32[96,1024]{1,0:T(8,128)S(1)} %get-tuple-element.27.refs_1_.refs_2_, ...), custom_call_target="tpu_custom_call", output_to_operand_aliasing={{0}: (8, {}), {1}: (9, {})} | custom-call | tf_op jit(solution)/shard_map/turn0/pallas_call | solution.py:438
  7.2 0.1 collective-permute-start.2
  7.3 1.2 %collective-permute-done.2.refs_0_ = f32[96,128]{1,0:T(8,128)S(1)} collective-permute-done((f32[96,128]{1,0:T(8,128)S(1)}, f32[96,128]{1,0:T(8,128)S(1)}, u32[]{:S(2)}, u32[]{:S(2)}) %collective-permute-start.2) | collective-permute-done | bytes 49184 | tf_op jit(solution)/shard_map/ppermute | solution.py:454
  8.5 1.7 %turn1.1 = (f32[96,1024]{1,0:T(8,128)S(1)}, f32[16,32,1024]{2,1,0:T(8,128)S(1)}, f32[96,128]{1,0:T(8,128)S(1)}) custom-call(f32[96,128]{1,0:T(8,128)S(1)} %collective-permute-done.2.refs_0_, f32[1,1024]{1,0:T(1,128)S(1)} %get-tuple-element.26.refs_0_.refs_1_.live, ...), custom_call_target="tpu_custom_call", output_to_operand_aliasing={{0}: (9, {}), {1}: (10, {})} | custom-call | tf_op jit(solution)/shard_map/turn1/pallas_call | solution.py:438
  10.2 3.4 %collective-permute-start.3 = (f32[96,128]{1,0:T(8,128)S(1)}, f32[96,128]{1,0:T(8,128)S(1)}, u32[]{:S(2)}, u32[]{:S(2)}) collective-permute-start(f32[96,128]{1,0:T(8,128)S(1)} %get-tuple-element.38), channel_id=1, source_target_pairs={{0,1},{1,0},{2,3},{3,2},{4,5},{5,4},{6,7},{7,6},{8,16},{9,17},{10,... | collective-permute-start | bytes 147464 | tf_op jit(solution)/shard_map/ppermute | solution.py:454
  13.7 2.1 %collective-permute-done.3.refs_0_ = f32[96,128]{1,0:T(8,128)S(1)} collective-permute-done((f32[96,128]{1,0:T(8,128)S(1)}, f32[96,128]{1,0:T(8,128)S(1)}, u32[]{:S(2)}, u32[]{:S(2)}) %collective-permute-start.3) | collective-permute-done | bytes 49184 | tf_op jit(solution)/shard_map/ppermute | solution.py:454
  15.8 1.8 %turn2.1 = (f32[96,1024]{1,0:T(8,128)S(1)}, f32[16,32,1024]{2,1,0:T(8,128)S(1)}, f32[96,128]{1,0:T(8,128)S(1)}) custom-call(f32[96,128]{1,0:T(8,128)S(1)} %collective-permute-done.3.refs_0_, f32[1,1024]{1,0:T(1,128)S(1)} %get-tuple-element.26.refs_0_.refs_1_.live, ...), custom_call_target="tpu_custom_call", output_to_operand_aliasing={{0}: (9, {}), {1}: (10, {})} | custom-call | tf_op jit(solution)/shard_map/turn2/pallas_call | solution.py:438
  17.6 0.1 collective-permute-start.4
  17.6 4.1 %collective-permute-done.4.refs_0_ = f32[96,128]{1,0:T(8,128)S(1)} collective-permute-done((f32[96,128]{1,0:T(8,128)S(1)}, f32[96,128]{1,0:T(8,128)S(1)}, u32[]{:S(2)}, u32[]{:S(2)}) %collective-permute-start.4) | collective-permute-done | bytes 49184 | tf_op jit(solution)/shard_map/ppermute | solution.py:454
  21.7 1.7 %turn3.1 = (f32[96,1024]{1,0:T(8,128)S(1)}, f32[16,32,1024]{2,1,0:T(8,128)S(1)}) custom-call(f32[96,128]{1,0:T(8,128)S(1)} %collective-permute-done.4.refs_0_, f32[1,1024]{1,0:T(1,128)S(1)} %get-tuple-element.26.refs_0_.refs_1_.live, f32[96,1024]{1,0:T(8,128)S(1)} %get-tuple-element.27.refs_1_.refs_2_, ...), custom_call_target="tpu_custom_call", output_to_operand_aliasing={{0}: (9, {}), {1}: (10, {})} | custom-call | tf_op jit(solution)/shard_map/turn3/pallas_call | solution.py:438
  23.4 2.5 %finish.1 = f32[16,32,1024]{2,1,0:T(8,128)} custom-call(f32[1,1024]{1,0:T(1,128)S(1)} %get-tuple-element.26.refs_0_.refs_1_.live, f32[96,1024]{1,0:T(8,128)S(1)} %get-tuple-element.44.e, f32[16,32,1024]{2,1,0:T(8,128)S(1)} %get-tuple-element.45.p, f32[48,1024]{1,0:T(8,128)S(1)} %get-tuple-element.46.il, ...), custom_call_target="tpu_custom_call" | custom-call | tf_op jit(solution)/shard_map/finish/pallas_call | solution.py:458
Async XLA Ops:
  0.0 5.3 %collective-permute-start.1 = (f32[2,96,128]{2,1,0:T(8,128)}, f32[2,96,128]{2,1,0:T(8,128)S(1)}, u32[]{:S(2)}, u32[]{:S(2)}) collective-permute-start(f32[2,96,128]{2,1,0:T(8,128)} %bitcast.16), channel_id=1, source_target_pairs={{0,8},{1,2},{2,1},{3,4},{4,3},{5,6},{6,5},{7,15},{8,0},{9,10},{10,... | collective-permute-start | bytes 294920 | tf_op jit(solution)/shard_map/ppermute | solution.py:375
  0.9 4.4 %collective-permute-start = (f32[2,96,128]{2,1,0:T(8,128)}, f32[2,96,128]{2,1,0:T(8,128)S(1)}, u32[]{:S(2)}, u32[]{:S(2)}) collective-permute-start(f32[2,96,128]{2,1,0:T(8,128)} %bitcast.17), channel_id=1, source_target_pairs={{0,1},{1,0},{2,3},{3,2},{4,5},{5,4},{6,7},{7,6},{8,9},{9,8},{10,11... | collective-permute-start | bytes 294920 | tf_op jit(solution)/shard_map/ppermute | solution.py:374
  7.2 1.3 %collective-permute-start.2 = (f32[96,128]{1,0:T(8,128)S(1)}, f32[96,128]{1,0:T(8,128)S(1)}, u32[]{:S(2)}, u32[]{:S(2)}) collective-permute-start(f32[96,128]{1,0:T(8,128)S(1)} %get-tuple-element.35), channel_id=1, source_target_pairs={{0,8},{1,9},{2,10},{3,11},{4,12},{5,13},{6,14},{7,15},{8,0},{9,1},... | collective-permute-start | bytes 147464 | tf_op jit(solution)/shard_map/ppermute | solution.py:454
  10.2 5.5 %collective-permute-start.3 = (f32[96,128]{1,0:T(8,128)S(1)}, f32[96,128]{1,0:T(8,128)S(1)}, u32[]{:S(2)}, u32[]{:S(2)}) collective-permute-start(f32[96,128]{1,0:T(8,128)S(1)} %get-tuple-element.38), channel_id=1, source_target_pairs={{0,1},{1,0},{2,3},{3,2},{4,5},{5,4},{6,7},{7,6},{8,16},{9,17},{10,... | collective-permute-start | bytes 147464 | tf_op jit(solution)/shard_map/ppermute | solution.py:454
  17.6 4.2 %collective-permute-start.4 = (f32[96,128]{1,0:T(8,128)S(1)}, f32[96,128]{1,0:T(8,128)S(1)}, u32[]{:S(2)}, u32[]{:S(2)}) collective-permute-start(f32[96,128]{1,0:T(8,128)S(1)} %get-tuple-element.41), channel_id=1, source_target_pairs={{0,1},{1,0},{2,3},{3,2},{4,5},{5,4},{6,7},{7,6},{8,9},{9,8},{10,11... | collective-permute-start | bytes 147464 | tf_op jit(solution)/shard_map/ppermute | solution.py:454

commit v2 on v1

v2 whole, which is shorter than its diff:
```python
import functools

import jax
import jax.numpy as jnp
from jax import lax
from jax.experimental import pallas as pl
from jax.experimental.pallas import tpu as pltpu
from jax.sharding import PartitionSpec as P

F32 = jnp.float32
BF16 = jnp.bfloat16
LANES = 128
SUB = 8
WROWS = 16
VM = pl.BlockSpec(memory_space=pltpu.VMEM)
HIGHEST = lax.Precision.HIGHEST


def params(mib):
    return pltpu.CompilerParams(vmem_limit_bytes=mib << 20)


def in_vmem(array):
    return pltpu.with_memory_space_constraint(array, pltpu.VMEM)


def in_hbm(array):
    return pltpu.with_memory_space_constraint(array, pltpu.HBM)


def split(values):
    high = values.astype(BF16)
    return high, (values - high.astype(F32)).astype(BF16)


def iota(shape, dim):
    return lax.broadcasted_iota(jnp.int32, shape, dim)


def coefficients(trace_map, lift_map, block):
    faces = trace_map.shape[0]
    width = block * block
    row = iota((block, width), 0)
    lane = iota((block, width), 1)
    first = lane // block == row
    second = lane % block == row
    spread_t = jnp.dot(trace_map, first.astype(F32), precision=HIGHEST)
    spread_l = jnp.dot(lift_map, second.astype(F32), precision=HIGHEST)
    rows = [jnp.where(second, spread_t[f : f + 1], 0.0) for f in range(faces)]
    rows += [jnp.where(first, spread_l[g : g + 1], 0.0) for g in range(faces)]
    rows += [spread_t[f : f + 1] * spread_l for f in range(faces)]
    rows.append(jnp.zeros((WROWS - faces * faces, width), F32))
    return jnp.concatenate(rows, axis=0)


def load(
    counts_hbm,
    inv_hbm,
    rhs_hbm,
    order_hbm,
    index_hbm,
    weights_hbm,
    trace_hbm,
    lift_hbm,
    ti,
    il,
    mix,
    q,
    inv,
    rhs,
    index,
    weights,
    live,
    p_out,
    carried_out,
    order,
    counts,
    trace_map,
    lift_map,
    sem,
):
    pairs = [
        (trace_hbm, trace_map),
        (lift_hbm, lift_map),
        (order_hbm, order),
        (inv_hbm, inv),
        (rhs_hbm, rhs),
        (index_hbm, index),
        (weights_hbm, weights),
        (counts_hbm, counts),
    ]
    copies = [pltpu.make_async_copy(a, b, sem.at[i]) for i, (a, b) in enumerate(pairs)]
    for copy in copies:
        copy.start()
    block, _, cells = inv.shape
    faces = trace_map.shape[0]
    for copy in copies[:3]:
        copy.wait()
    high, low = split(coefficients(trace_map[...], lift_map[...], block))
    for j in range(cells // LANES):
        hit = iota((LANES, cells), 0) + j * LANES == order[...]
        q[j * LANES : (j + 1) * LANES, :] = jnp.where(hit, 1.0, 0.0).astype(BF16)
    copies[7].wait()
    for level in range(cells // LANES):
        here = iota((1, LANES), 1) < counts[level]
        live[:, level * LANES : (level + 1) * LANES] = here.astype(F32)
    copies[3].wait()
    flat = inv[...].reshape(block * block, cells)
    made = jnp.dot(high, flat, preferred_element_type=F32) + jnp.dot(
        low, flat, preferred_element_type=F32
    )
    ti[...] = made[: faces * block]
    il[...] = made[faces * block : 2 * faces * block]
    high, low = split(made[2 * faces * block :])
    mix[:WROWS, :] = high
    mix[WROWS:, :] = low
    for copy in copies[4:7]:
        copy.wait()


def local_first(*refs, axes):
    flow, cross = axes

    @pl.when(lax.axis_index(flow) == 0)
    def _():
        local_work(*refs, cross=cross, first=True)


def local_rest(*refs, axes):
    flow, cross = axes
    order, qt = refs[9], refs[18]
    cells = qt.shape[0]
    for level in range(cells // LANES):
        at = slice(level * LANES, (level + 1) * LANES)
        spread = jnp.broadcast_to(order[:, at].astype(F32), (LANES, LANES)).T
        for j in range(cells // LANES):
            hit = spread == (iota((LANES, LANES), 1) + j * LANES).astype(F32)
            qt[at, j * LANES : (j + 1) * LANES] = jnp.where(hit, 1.0, 0.0).astype(BF16)

    @pl.when(lax.axis_index(flow) > 0)
    def _():
        local_work(*refs[:9], *refs[14:18], *refs[19:], cross=cross, first=False)


def local_work(
    ring_a,
    ring_b,
    ti,
    mix,
    rhs,
    q,
    live,
    index,
    weights,
    r_out,
    w_out,
    e_out,
    s_out,
    stacked,
    rim,
    *,
    cross,
    first,
):
    block, tracers, cells = rhs.shape
    rows = r_out.shape[0]
    faces = rows // tracers
    half = rows + WROWS
    stacked[rows:half, :] = mix[:WROWS, :]
    stacked[half + rows :, :] = mix[WROWS:, :]
    rim_sources(ring_a, ring_b, rim, cross)
    groups = cells // LANES
    slots = None
    for j in range(groups):
        at = pl.ds(j * LANES, LANES)
        sums = [None] * faces
        for b in range(block):
            source = rhs[b, :, at].astype(F32)
            for f in range(faces):
                term = ti[f * block + b : f * block + b + 1, at] * source
                sums[f] = term if sums[f] is None else sums[f] + term
        for f in range(faces):
            high, low = split(sums[f])
            stacked[f * tracers : (f + 1) * tracers, at] = high
            stacked[half + f * tracers : half + (f + 1) * tracers, at] = low
        rim_level(j, rim, index, weights, e_out)
        if (j + 1) % (groups // 2) == 0:
            part = pl.ds((j + 1 - groups // 2) * LANES, groups // 2 * LANES)
            term = jnp.dot(stacked[:, part], q[part, :], preferred_element_type=F32)
            slots = term if slots is None else slots + term
    slots = slots[:half] + slots[half:]
    r_out[...] = slots[:rows] * live[...]
    w_out[...] = slots[rows:] * live[...]
    if not first:
        for level in range(groups):
            inflow_weights(level, index, weights, s_out)


def gathered(source, lane):
    return jnp.take_along_axis(source, lane, axis=1, mode="promise_in_bounds")


def face_values(faces_at, level, sources, index, count):
    at = index[faces_at : faces_at + 1, level * LANES : (level + 1) * LANES]
    at = jnp.broadcast_to(at, (SUB, LANES))
    lane = at & (LANES - 1)
    group = lax.shift_right_logical(at, LANES.bit_length() - 1)
    values = [None] * count
    for code, read in sources:
        here = group == code
        for i in range(count):
            got = gathered(read(i), lane)
            values[i] = jnp.where(here, got, 0.0 if values[i] is None else values[i])
    return values


def rows_of(i):
    return slice(i * SUB, (i + 1) * SUB)


def inflow_only(face, level):
    return face == 1 or (face == 0 and level == 0)


def rim_sources(ring_a, ring_b, rim, cross):
    column = lax.axis_index(cross)
    last = lax.axis_size(cross) - 1
    even = column % 2 == 0
    lower = jnp.where(even, ring_b[1], ring_a[1])
    upper = jnp.where(even, ring_a[0], ring_b[0])
    rim[0] = jnp.where(column > 0, lower, 0.0)
    rim[1] = jnp.where(column < last, upper, 0.0)


def rim_level(level, rim, index, weights, e_out):
    count = e_out.shape[0] // SUB
    at = slice(level * LANES, (level + 1) * LANES)
    sums = [None] * count
    for face in range(index.shape[0]):
        if inflow_only(face, level):
            continue
        sources = [(1 + s, lambda i, s=s: rim[s, rows_of(i), :]) for s in range(2)]
        values = face_values(face, level, sources, index, count)
        weight = jnp.broadcast_to(weights[face : face + 1, at], (SUB, LANES))
        for i in range(count):
            term = values[i] * weight
            sums[i] = term if sums[i] is None else sums[i] + term
    for i in range(count):
        e_out[rows_of(i), at] = sums[i]


def inflow_weights(level, index, weights, s_out):
    at = slice(level * LANES, (level + 1) * LANES)
    source = iota((LANES, LANES), 0)
    total = None
    for face in range(index.shape[0]):
        hit = index[face : face + 1, at] == source
        term = jnp.where(hit, weights[face : face + 1, at], 0.0)
        total = term if total is None else total + term
    high, low = split(total)
    s_out[:, at] = high
    s_out[:, slice(s_out.shape[1] // 2 + at.start, s_out.shape[1] // 2 + at.stop)] = low


def sweep(
    inflow, live, r, w, index, weights, s, e, qt, back, traces_out, pool, ends, stacked, face_dofs
):
    faces, cells = index.shape
    levels = cells // LANES
    rows = e.shape[0]
    count = rows // SUB
    per_dof = count // face_dofs
    pair = 2 * LANES
    if inflow is not None:
        high, low = split(inflow[...])
        ends[:rows, :] = high
        ends[rows:, :] = low
    for level in range(levels):
        at = slice(level * LANES, (level + 1) * LANES)
        if inflow is not None and level % 2 == 0:
            both = slice(level * LANES, level * LANES + pair)
            main = jnp.dot(ends[...], s[:, both], preferred_element_type=F32)
            rest = jnp.dot(
                ends[:rows, :],
                s[:, slice(cells + both.start, cells + both.stop)],
                preferred_element_type=F32,
            )
            given = e[:, both] + (main[:rows] + (main[rows:] + rest))
        if inflow is None:
            sums = [e[rows_of(i), at] for i in range(count)]
        else:
            half = slice(level % 2 * LANES, (level % 2 + 1) * LANES)
            sums = [given[rows_of(i), half] for i in range(count)]
        for face in range(faces):
            if inflow_only(face, level) or level == 0:
                continue
            sources = [(3 + v, lambda i, v=v: pool[v, rows_of(i), :]) for v in range(level)]
            values = face_values(face, level, sources, index, count)
            weight = jnp.broadcast_to(weights[face : face + 1, at], (SUB, LANES))
            for i in range(count):
                sums[i] = sums[i] + values[i] * weight
        spot = at
        for i in range(0, count, 2):
            masked = jnp.concatenate([sums[i], sums[i + 1]], axis=0) * live[:, at]
            high, low = split(masked)
            stacked[i * SUB : (i + 2) * SUB, spot] = high
            stacked[rows + i * SUB : rows + (i + 2) * SUB, spot] = low
        for f in range(face_dofs):
            mix = [
                jnp.broadcast_to(w[face_dofs * f + g : face_dofs * f + g + 1, at], (SUB, LANES))
                for g in range(face_dofs)
            ]
            for k in range(per_dof):
                i = f * per_dof + k
                value = r[rows_of(i), at]
                for g in range(face_dofs):
                    value = value + mix[g] * sums[g * per_dof + k]
                if level < levels - 1:
                    pool[level, rows_of(i), :] = value
                else:
                    traces_out[rows_of(i), :] = value
        if back is not None and level % 2 == 1:
            both = slice((level - 1) * LANES, (level + 1) * LANES)
            moved = jnp.dot(stacked[:, both], qt[both, :], preferred_element_type=F32)
            moved = moved[:rows] + moved[rows:]
            back[...] = moved if level == 1 else back[...] + moved


def local_group(j, live, inv, rhs, q, p_out, wide):
    block = inv.shape[0]
    cells = rhs.shape[2]
    start = pl.multiple_of(j * LANES, LANES)
    at = pl.ds(start, LANES)
    rows = jnp.broadcast_to(live[...], (WROWS, cells)).astype(BF16)
    mask = lax.dot_general(
        rows, q[at, :], (((1,), (1,)), ((), ())), preferred_element_type=F32
    )[:1]
    for a in range(block):
        wide[a * block : (a + 1) * block, :] = inv[a, :, at].astype(F32) * mask
    step = 4

    def some(part, carry):
        sums = [None] * step
        for b in range(block):
            source = rhs[b, :, at].astype(F32)
            for i in range(step):
                row = (part * step + i) * block + b
                term = wide[pl.ds(row, 1), :] * source
                sums[i] = term if sums[i] is None else sums[i] + term
        for i in range(step):
            p_out[part * step + i, :, at] = sums[i]
        return carry

    lax.fori_loop(0, block // step, some, 0)


def local_plan(flows, groups):
    plan = []
    for f in range(flows):
        steps = [("turn", m) for m in range(f) if (f, m) != (1, 0)]
        steps += [("window", m) for m in range(max(f, min(1, flows - 2)), flows - 1)]
        steps = steps or [("final", flows - 1)]
        ends = [-(-k * groups // len(steps)) for k in range(len(steps) + 1)]
        plan.append({step: (ends[k], ends[k + 1]) for k, step in enumerate(steps)})
    return plan


def planned_groups(step, flow, live, inv, rhs, q, p_out, wide):
    flows = lax.axis_size(flow)
    plan = local_plan(flows, rhs.shape[2] // LANES)
    if not any(step in own for own in plan):
        return
    position = lax.axis_index(flow)
    first = end = 0
    for f in range(flows):
        low, high = plan[f].get(step, (0, 0))
        first = jnp.where(position == f, low, first)
        end = jnp.where(position == f, high, end)
    lax.fori_loop(
        first, end, lambda j, c: (local_group(j, live, inv, rhs, q, p_out, wide), c)[1], 0
    )


def turn(*refs, moment, flow, face_dofs, fused):
    refs = list(refs)
    inflow = refs.pop(0) if moment > 0 else None
    live, r, w, index, weights, e = refs[:6]
    refs = refs[6:]
    s = qt = ends = back = None
    if moment > 0:
        s, qt = refs[:2]
        refs = refs[2:]
    if fused:
        back, traces_out, stacked, pool, ends = refs
    else:
        inv, rhs, q, _, _, p_out, stacked, traces_out, pool, wide = refs[:10]
        ends = refs[10] if moment > 0 else None

    @pl.when(lax.axis_index(flow) == moment)
    def _():
        sweep(
            inflow,
            live,
            r,
            w,
            index,
            weights,
            s,
            e,
            qt,
            back,
            traces_out,
            pool,
            ends,
            stacked,
            face_dofs,
        )

    if not fused:
        planned_groups(("turn", moment), flow, live, inv, rhs, q, p_out, wide)


def window(live, inv, rhs, q, _, p_out, wide, *, moment, flow):
    planned_groups(("window", moment), flow, live, inv, rhs, q, p_out, wide)


def move_back(carried, qt, back):
    moved = jnp.dot(carried[...], qt[...], preferred_element_type=F32)
    rows = back.shape[0]
    back[...] = moved[:rows] + moved[rows:]


def early(live, inv, rhs, q, carried, qt, il, _, p, out, wide, back, done, sem, *, moment, flow):
    planned_groups(("window", moment), flow, live, inv, rhs, q, p, wide)

    @pl.when(lax.axis_index(flow) <= moment)
    def _():
        move_back(carried, qt, back)
        write_solution(back, p, il, out, done, sem)


def final(live, inv, rhs, q, back, qt, il, _, out_in, p, out, wide, moved, done, sem, *, flow, fused):
    last = lax.axis_size(flow) - 1
    planned_groups(("final", last), flow, live, inv, rhs, q, p, wide)

    @pl.when(lax.axis_index(flow) == last)
    def _():
        if not fused:
            move_back(back, qt, moved)
        write_solution(back if fused else moved, p, il, out, done, sem)


def write_solution(back, p, il, out, done, sem):
    block, tracers, cells = p.shape
    face_dofs = back.shape[0] // tracers
    copies = []
    for a in range(block):
        for j in range(cells // LANES):
            at = pl.ds(j * LANES, LANES)
            value = p[a, :, at]
            for g in range(face_dofs):
                scale = il[g * block + a : g * block + a + 1, at]
                value = value + scale * back[g * tracers : (g + 1) * tracers, at]
            done[a, :, at] = value
        copy = pltpu.make_async_copy(done.at[a], out.at[a], sem.at[a])
        copy.start()
        copies.append(copy)
    for copy in copies:
        copy.wait()


def swaps(flows, columns, partner):
    pairs = []
    for f in range(flows):
        for c in range(columns):
            to_f, to_c = partner(f, c)
            if not (0 <= to_f < flows and 0 <= to_c < columns):
                to_f, to_c = f, c
            pairs.append((f * columns + c, to_f * columns + to_c))
    return pairs


def rim_partner(first, columns):
    def partner(f, c):
        other = c + 1 if c % 2 == first else c - 1
        if columns % 2 == 0:
            other %= columns
        return f, other

    return partner


def hop_partner(moment):
    def partner(f, c):
        return (2 * moment + 1 - f, c) if f in (moment, moment + 1) else (f, c ^ 1)

    return partner


def shards(
    rhs,
    inverses,
    flux_weights,
    upwind_index,
    sweep_order,
    level_counts,
    boundary_traces,
    trace_map,
    lift_map,
):
    _, _, block, tracers, cells = rhs.shape
    face_dofs = trace_map.shape[0]
    rows = face_dofs * tracers
    flows = lax.axis_size("flow")
    columns = lax.axis_size("cross")
    edges = boundary_traces.reshape(2, rows, LANES)
    axes = ("flow", "cross")
    ring_a = lax.ppermute(edges, axes, swaps(flows, columns, rim_partner(0, columns)))
    ring_b = lax.ppermute(edges, axes, swaps(flows, columns, rim_partner(1, columns)))
    faces = upwind_index.shape[2]
    far = pl.BlockSpec(memory_space=pltpu.HBM)

    ti, il, mix, q, inv, rhs, index, weights, live, p, carried, order = pl.pallas_call(
        load,
        out_shape=(
            pltpu.VMEM((face_dofs * block, cells), F32),
            pltpu.VMEM((face_dofs * block, cells), F32),
            pltpu.VMEM((2 * WROWS, cells), BF16),
            pltpu.VMEM((cells, cells), BF16),
            pltpu.VMEM((block, block, cells), BF16),
            pltpu.VMEM((block, tracers, cells), BF16),
            pltpu.VMEM((faces, cells), jnp.int32),
            pltpu.VMEM((faces, cells), F32),
            pltpu.VMEM((1, cells), F32),
            pltpu.VMEM((block, tracers, cells), F32),
            pltpu.VMEM((2 * rows, cells), BF16),
            pltpu.VMEM((1, cells), jnp.int32),
        ),
        in_specs=[far] * 8,
        out_specs=(VM,) * 12,
        scratch_shapes=[
            pltpu.SMEM((cells // LANES,), jnp.int32),
            pltpu.VMEM((face_dofs, block), F32),
            pltpu.VMEM((face_dofs, block), F32),
            pltpu.SemaphoreType.DMA((8,)),
        ],
        compiler_params=params(12),
        name="load",
    )(
        in_hbm(level_counts[0, 0]),
        in_hbm(inverses[0, 0]),
        in_hbm(rhs[0, 0]),
        in_hbm(sweep_order[0]),
        in_hbm(upwind_index[0, 0]),
        in_hbm(flux_weights[0, 0]),
        in_hbm(trace_map),
        in_hbm(lift_map.T),
    )

    made_shapes = [
        pltpu.VMEM((rows, cells), F32),
        pltpu.VMEM((WROWS, cells), F32),
        pltpu.VMEM((rows, cells), F32),
        pltpu.VMEM((LANES, 2 * cells), BF16),
    ]
    local_scratch = [
        pltpu.VMEM((2 * (rows + WROWS), cells), BF16),
        pltpu.VMEM((2, rows, LANES), F32),
    ]
    local_given = [in_vmem(ring_a), in_vmem(ring_b), ti, mix, rhs, q, live, index, weights]
    r, w, e, s = pl.pallas_call(
        functools.partial(local_first, axes=axes),
        out_shape=made_shapes,
        in_specs=[VM] * 9,
        out_specs=[VM] * 4,
        scratch_shapes=local_scratch,
        compiler_params=params(12),
        name="local_first",
    )(*local_given)

    back_shape = pltpu.VMEM((rows, cells), F32)
    p_shape = pltpu.VMEM((block, tracers, cells), F32)
    halves = pltpu.VMEM((2 * rows, cells), BF16)
    sent = pltpu.VMEM((rows, LANES), F32)
    pool = pltpu.VMEM((cells // LANES, rows, LANES), F32)
    wide = pltpu.VMEM((block * block, LANES), F32)
    ends = pltpu.VMEM((2 * rows, LANES), BF16)
    out_shape = pltpu.HBM((block, tracers, cells), F32)
    out_scratch = [p_shape, pltpu.SemaphoreType.DMA((block,))]
    qt = received = out = back = None
    for moment in range(flows):
        last = moment == flows - 1
        fused = last and moment > 0
        given = [] if moment == 0 else [in_vmem(received)]
        given += [live, r, w, index, weights, e] + ([] if moment == 0 else [s, qt])
        more = [] if moment == 0 else [ends]
        run = functools.partial(
            turn, moment=moment, flow="flow", face_dofs=face_dofs, fused=fused
        )
        if fused:
            back = pl.pallas_call(
                run,
                out_shape=back_shape,
                in_specs=[VM] * len(given),
                out_specs=VM,
                scratch_shapes=[sent, halves, pool, ends],
                compiler_params=params(4),
                name=f"turn{moment}",
            )(*given)
            break
        given += [inv, rhs, q, p, carried]
        p, carried, traces = pl.pallas_call(
            run,
            out_shape=[p_shape, halves, sent],
            in_specs=[VM] * len(given),
            out_specs=[VM] * 3,
            input_output_aliases={len(given) - 2: 0, len(given) - 1: 1},
            scratch_shapes=[pool, wide] + more,
            compiler_params=params(4),
            name=f"turn{moment}",
        )(*given)
        if not last:
            received = lax.ppermute(traces, axes, swaps(flows, columns, hop_partner(moment)))
        if moment == 0:
            r, w, e, s, qt = pl.pallas_call(
                functools.partial(local_rest, axes=axes),
                out_shape=made_shapes + [pltpu.VMEM((cells, cells), BF16)],
                in_specs=[VM] * 14,
                out_specs=[VM] * 5,
                input_output_aliases={10: 0, 11: 1, 12: 2, 13: 3},
                scratch_shapes=local_scratch,
                compiler_params=params(12),
                name="local_rest",
            )(*local_given, order, r, w, e, s)
        if moment == flows - 2:
            p, out = pl.pallas_call(
                functools.partial(early, moment=moment, flow="flow"),
                out_shape=[p_shape, out_shape],
                in_specs=[VM] * 8,
                out_specs=[VM, far],
                input_output_aliases={7: 0},
                scratch_shapes=[wide, back_shape] + out_scratch,
                compiler_params=params(8),
                name="early",
            )(live, inv, rhs, q, carried, qt, il, p)
        elif 0 < moment < flows - 2:
            p = pl.pallas_call(
                functools.partial(window, moment=moment, flow="flow"),
                out_shape=p_shape,
                in_specs=[VM] * 5,
                out_specs=VM,
                input_output_aliases={4: 0},
                scratch_shapes=[wide],
                compiler_params=params(4),
                name=f"window{moment}",
            )(live, inv, rhs, q, p)

    if out is None:
        out = jnp.zeros((block, tracers, cells), F32)
    p, out = pl.pallas_call(
        functools.partial(final, flow="flow", fused=fused),
        out_shape=[p_shape, out_shape],
        in_specs=[VM] * 8 + [far],
        out_specs=[VM, far],
        input_output_aliases={7: 0, 8: 1},
        scratch_shapes=[wide, back_shape] + out_scratch,
        compiler_params=params(8),
        name="final",
    )(live, inv, rhs, q, back if fused else carried, qt, il, p, out)
    return out[None, None]


def solution(mesh):
    placed = (
        P("flow", "cross", None, None, None),
        P("flow", "cross", None, None, None),
        P("flow", "cross", None, None),
        P("flow", "cross", None, None),
        P("flow", "cross", None),
        P("flow", "cross", None),
        P("flow", "cross", None, None, None),
        P(),
        P(),
    )
    return jax.shard_map(
        shards,
        mesh=mesh,
        in_specs=placed,
        out_specs=P("flow", "cross", None, None, None),
        check_vma=False,
    )
```

time: 26.1 us -> 24.1 us (0.923)
  the two profiles are of different devices: /device:TPU:20 before, /device:TPU:26 now
where the time goes in v2:
time: 24.1 us; the launch traced here: 23.8 us
  Pallas kernels  12.3 us (51%)
  starting transfers between devices  7.27 us (30%)
  waiting for transfers between devices  4.15 us (17%)
    ppermute x3, starting transfers between devices, shards(): lax.ppermute(traces, axes, swaps(flows, columns, hop_partner(moment)))  5.66 us
    pallas_call x3, Pallas kernels, shards(): pl.pallas_call(run, out_shape=[p_shape, halves, sent], in_specs=[VM] * le...  4.61 us
    ppermute x3, waiting for transfers between devices, shards(): lax.ppermute(traces, axes, swaps(flows, columns, hop_partner(moment)))  3.11 us
    pallas_call x1, Pallas kernels, shards(): pl.pallas_call(functools.partial(local_rest, axes=axes), out_shape=made_s...  2.19 us
    pallas_call x1, Pallas kernels, shards(): pl.pallas_call(run, out_shape=back_shape, in_specs=[VM] * len(given), out...  2.17 us
    pallas_call x1, Pallas kernels, shards(): pl.pallas_call(load, out_shape=(pltpu.VMEM((face_dofs * block, cells), F3...  1.69 us
    ppermute x1, starting transfers between devices, shards(): lax.ppermute(edges, axes, swaps(flows, columns, rim_partner(0, columns)))  1.6 us
    pallas_call x1, Pallas kernels, shards(): pl.pallas_call(functools.partial(final, flow='flow', fused=fused), out_sh...  1.51 us
  transfers between devices with their start and end apart: 5, of which 3 were waited for; matrix products, arithmetic and copies ran while one was open for 0% of the time, Pallas kernels for 17%

profile of v2, /device:TPU:26, one launch (start us, length us, event | category | flops | bytes accessed | tf_op | source)
XLA Modules:
  0.0 23.8 jit_solution(4833594101485738336)
XLA Ops:
  0.0 0.0 collective-permute-start.1
  0.0 1.6 %collective-permute-start = (f32[2,96,128]{2,1,0:T(8,128)}, f32[2,96,128]{2,1,0:T(8,128)S(1)}, u32[]{:S(2)}, u32[]{:S(2)}) collective-permute-start(f32[2,96,128]{2,1,0:T(8,128)} %bitcast.17), channel_id=1, source_target_pairs={{0,1},{1,0},{2,3},{3,2},{4,5},{5,4},{6,7},{7,6},{8,9},{9,8},{10,11... | collective-permute-start | bytes 294920 | tf_op jit(solution)/shard_map/ppermute | solution.py:518
  1.6 1.7 %load.1 = (f32[48,1024]{1,0:T(8,128)S(1)}, f32[48,1024]{1,0:T(8,128)S(1)}, bf16[32,1024]{1,0:T(8,128)(2,1)S(1)}, bf16[1024,1024]{1,0:T(8,128)(2,1)S(1)}, bf16[16...) custom-call(s32[8]{0:T(128)} %bitcast.15, ...), custom_call_target="tpu_custom_call" | custom-call | tf_op jit(solution)/shard_map/load/pallas_call | solution.py:523
  3.3 1.0 %collective-permute-done.1.refs_1_ = f32[2,96,128]{2,1,0:T(8,128)S(1)} collective-permute-done((f32[2,96,128]{2,1,0:T(8,128)}, f32[2,96,128]{2,1,0:T(8,128)S(1)}, u32[]{:S(2)}, u32[]{:S(2)}) %collective-permute-start.1) | collective-permute-done | bytes 98336 | tf_op jit(solution)/shard_map/ppermute | solution.py:519
  4.3 0.0 collective-permute-done.refs_0_
  4.3 1.7 %turn0.1 = (f32[16,32,1024]{2,1,0:T(8,128)S(1)}, bf16[192,1024]{1,0:T(8,128)(2,1)S(1)}, f32[96,128]{1,0:T(8,128)S(1)}) custom-call(f32[1,1024]{1,0:T(1,128)S(1)} %get-tuple-element.38.refs_6_.refs_0_.refs_1_.live, f32[96,1024]{1,0:T(8,128)S(1)} %get-tuple-element.46.refs_1_.refs_10_, ...), custom_call_target="tpu_custom_call", output_to_operand_aliasing={{0}: (9, {}), {1}: (10, {})} | custom-call | tf_op jit(solution)/shard_map/turn0/pallas_call | solution.py:612
  6.1 1.7 %collective-permute-start.2 = (f32[96,128]{1,0:T(8,128)S(1)}, f32[96,128]{1,0:T(8,128)S(1)}, u32[]{:S(2)}, u32[]{:S(2)}) collective-permute-start(f32[96,128]{1,0:T(8,128)S(1)} %get-tuple-element.51), channel_id=1, source_target_pairs={{0,8},{1,9},{2,10},{3,11},{4,12},{5,13},{6,14},{7,15},{8,0},{9,1},... | collective-permute-start | bytes 147464 | tf_op jit(solution)/shard_map/ppermute | solution.py:623
  7.8 2.2 %local_rest.1 = (f32[96,1024]{1,0:T(8,128)S(1)}, f32[16,1024]{1,0:T(8,128)S(1)}, f32[96,1024]{1,0:T(8,128)S(1)}, bf16[128,2048]{1,0:T(8,128)(2,1)S(1)}, bf16[1024,1024]{1,0:T(8,128)(2,1)S(1)}) custom-call(f32[2,96,128]{2,1,0:T(8,128)S(1)} %collective-permute-done.refs_0_, ...), custom_call_target="tpu_custom_call", output_to_operand_aliasing={{0}: (10, {}), {1}: (11, {}), {2}: (12, {}), {3}: (13, {})} | custom-call | tf_op jit(solution)/shard_map/local_rest/pallas_call | solution.py:625
  10.0 0.0 collective-permute-done.2.refs_0_
  10.0 1.7 %turn1.1 = (f32[16,32,1024]{2,1,0:T(8,128)S(1)}, bf16[192,1024]{1,0:T(8,128)(2,1)S(1)}, f32[96,128]{1,0:T(8,128)S(1)}) custom-call(f32[96,128]{1,0:T(8,128)S(1)} %collective-permute-done.2.refs_0_, f32[1,1024]{1,0:T(1,128)S(1)} %get-tuple-element.38.refs_6_.refs_0_.refs_1_.live, ...), custom_call_target="tpu_custom_call", output_to_operand_aliasing={{0}: (12, {}), {1}: (13, {})} | custom-call | tf_op jit(solution)/shard_map/turn1/pallas_call | solution.py:612
  11.7 0.1 collective-permute-start.3
  11.9 1.2 %collective-permute-done.3.refs_0_ = f32[96,128]{1,0:T(8,128)S(1)} collective-permute-done((f32[96,128]{1,0:T(8,128)S(1)}, f32[96,128]{1,0:T(8,128)S(1)}, u32[]{:S(2)}, u32[]{:S(2)}) %collective-permute-start.3) | collective-permute-done | bytes 49184 | tf_op jit(solution)/shard_map/ppermute | solution.py:623
  13.0 1.1 %turn2.1 = (f32[16,32,1024]{2,1,0:T(8,128)S(1)}, bf16[192,1024]{1,0:T(8,128)(2,1)S(1)}, f32[96,128]{1,0:T(8,128)S(1)}) custom-call(f32[96,128]{1,0:T(8,128)S(1)} %collective-permute-done.3.refs_0_, f32[1,1024]{1,0:T(1,128)S(1)} %get-tuple-element.38.refs_6_.refs_0_.refs_1_.live, ...), custom_call_target="tpu_custom_call", output_to_operand_aliasing={{0}: (12, {}), {1}: (13, {})} | custom-call | tf_op jit(solution)/shard_map/turn2/pallas_call | solution.py:612
  14.2 3.9 %collective-permute-start.4 = (f32[96,128]{1,0:T(8,128)S(1)}, f32[96,128]{1,0:T(8,128)S(1)}, u32[]{:S(2)}, u32[]{:S(2)}) collective-permute-start(f32[96,128]{1,0:T(8,128)S(1)} %get-tuple-element.64), channel_id=1, source_target_pairs={{0,1},{1,0},{2,3},{3,2},{4,5},{5,4},{6,7},{7,6},{8,9},{9,8},{10,11... | collective-permute-start | bytes 147464 | tf_op jit(solution)/shard_map/ppermute | solution.py:623
  18.1 0.1 early.1
  18.2 1.9 %collective-permute-done.4.refs_0_ = f32[96,128]{1,0:T(8,128)S(1)} collective-permute-done((f32[96,128]{1,0:T(8,128)S(1)}, f32[96,128]{1,0:T(8,128)S(1)}, u32[]{:S(2)}, u32[]{:S(2)}) %collective-permute-start.4) | collective-permute-done | bytes 49184 | tf_op jit(solution)/shard_map/ppermute | solution.py:623
  20.1 2.2 %turn3.1.back = f32[96,1024]{1,0:T(8,128)S(1)} custom-call(f32[96,128]{1,0:T(8,128)S(1)} %collective-permute-done.4.refs_0_, f32[1,1024]{1,0:T(1,128)S(1)} %get-tuple-element.38.refs_6_.refs_0_.refs_1_.live, f32[96,1024]{1,0:T(8,128)S(1)} %get-tuple-element.54.refs_2_, f32[16,1024]{1,0:T(8,128)S(1)} %get-tuple-element.55.refs_3_, ...), custom_call_target="tpu_custom_call" | custom-call | tf_op jit(solution)/shard_map/turn3/pallas_call | solution.py:601
  22.3 1.5 %final.1 = (f32[16,32,1024]{2,1,0:T(8,128)S(1)}, f32[16,32,1024]{2,1,0:T(8,128)}) custom-call(f32[1,1024]{1,0:T(1,128)S(1)} %get-tuple-element.38.refs_6_.refs_0_.refs_1_.live, bf16[16,16,1024]{2,1,0:T(8,128)(2,1)S(1)} %get-tuple-element.39.refs_6_.refs_9_.inv, ...), custom_call_target="tpu_custom_call", output_to_operand_aliasing={{0}: (7, {}), {1}: (8, {})} | custom-call | tf_op jit(solution)/shard_map/final/pallas_call | solution.py:660
  (2 shorter events, 0.0 us)
Async XLA Ops:
  0.0 4.3 %collective-permute-start.1 = (f32[2,96,128]{2,1,0:T(8,128)}, f32[2,96,128]{2,1,0:T(8,128)S(1)}, u32[]{:S(2)}, u32[]{:S(2)}) collective-permute-start(f32[2,96,128]{2,1,0:T(8,128)} %bitcast.16), channel_id=1, source_target_pairs={{0,7},{1,2},{2,1},{3,4},{4,3},{5,6},{6,5},{7,0},{8,15},{9,10},{10,... | collective-permute-start | bytes 294920 | tf_op jit(solution)/shard_map/ppermute | solution.py:519
  0.0 4.3 %collective-permute-start = (f32[2,96,128]{2,1,0:T(8,128)}, f32[2,96,128]{2,1,0:T(8,128)S(1)}, u32[]{:S(2)}, u32[]{:S(2)}) collective-permute-start(f32[2,96,128]{2,1,0:T(8,128)} %bitcast.17), channel_id=1, source_target_pairs={{0,1},{1,0},{2,3},{3,2},{4,5},{5,4},{6,7},{7,6},{8,9},{9,8},{10,11... | collective-permute-start | bytes 294920 | tf_op jit(solution)/shard_map/ppermute | solution.py:518
  6.1 3.9 %collective-permute-start.2 = (f32[96,128]{1,0:T(8,128)S(1)}, f32[96,128]{1,0:T(8,128)S(1)}, u32[]{:S(2)}, u32[]{:S(2)}) collective-permute-start(f32[96,128]{1,0:T(8,128)S(1)} %get-tuple-element.51), channel_id=1, source_target_pairs={{0,8},{1,9},{2,10},{3,11},{4,12},{5,13},{6,14},{7,15},{8,0},{9,1},... | collective-permute-start | bytes 147464 | tf_op jit(solution)/shard_map/ppermute | solution.py:623
  11.7 1.3 %collective-permute-start.3 = (f32[96,128]{1,0:T(8,128)S(1)}, f32[96,128]{1,0:T(8,128)S(1)}, u32[]{:S(2)}, u32[]{:S(2)}) collective-permute-start(f32[96,128]{1,0:T(8,128)S(1)} %get-tuple-element.61), channel_id=1, source_target_pairs={{0,1},{1,0},{2,3},{3,2},{4,5},{5,4},{6,7},{7,6},{8,16},{9,17},{10,... | collective-permute-start | bytes 147464 | tf_op jit(solution)/shard_map/ppermute | solution.py:623
  14.2 5.9 %collective-permute-start.4 = (f32[96,128]{1,0:T(8,128)S(1)}, f32[96,128]{1,0:T(8,128)S(1)}, u32[]{:S(2)}, u32[]{:S(2)}) collective-permute-start(f32[96,128]{1,0:T(8,128)S(1)} %get-tuple-element.64), channel_id=1, source_target_pairs={{0,1},{1,0},{2,3},{3,2},{4,5},{5,4},{6,7},{7,6},{8,9},{9,8},{10,11... | collective-permute-start | bytes 147464 | tf_op jit(solution)/shard_map/ppermute | solution.py:623

commit v3 on v2

--- a/solution.py
+++ b/solution.py
@@ -12,6 +12,7 @@
 LANES = 128
 SUB = 8
 WROWS = 16
+LAG = 3
 VM = pl.BlockSpec(memory_space=pltpu.VMEM)
 HIGHEST = lax.Precision.HIGHEST
 
@@ -118,57 +119,13 @@
         copy.wait()
 
 
-def local_first(*refs, axes):
-    flow, cross = axes
-
-    @pl.when(lax.axis_index(flow) == 0)
-    def _():
-        local_work(*refs, cross=cross, first=True)
-
-
-def local_rest(*refs, axes):
-    flow, cross = axes
-    order, qt = refs[9], refs[18]
-    cells = qt.shape[0]
-    for level in range(cells // LANES):
-        at = slice(level * LANES, (level + 1) * LANES)
-        spread = jnp.broadcast_to(order[:, at].astype(F32), (LANES, LANES)).T
-        for j in range(cells // LANES):
-            hit = spread == (iota((LANES, LANES), 1) + j * LANES).astype(F32)
-            qt[at, j * LANES : (j + 1) * LANES] = jnp.where(hit, 1.0, 0.0).astype(BF16)
-
-    @pl.when(lax.axis_index(flow) > 0)
-    def _():
-        local_work(*refs[:9], *refs[14:18], *refs[19:], cross=cross, first=False)
-
-
-def local_work(
-    ring_a,
-    ring_b,
-    ti,
-    mix,
-    rhs,
-    q,
-    live,
-    index,
-    weights,
-    r_out,
-    w_out,
-    e_out,
-    s_out,
-    stacked,
-    rim,
-    *,
-    cross,
-    first,
-):
+def products(ti, mix, rhs, q, live, r_out, w_out, stacked):
     block, tracers, cells = rhs.shape
     rows = r_out.shape[0]
     faces = rows // tracers
     half = rows + WROWS
     stacked[rows:half, :] = mix[:WROWS, :]
     stacked[half + rows :, :] = mix[WROWS:, :]
-    rim_sources(ring_a, ring_b, rim, cross)
     groups = cells // LANES
     slots = None
     for j in range(groups):
@@ -183,7 +140,6 @@
             high, low = split(sums[f])
             stacked[f * tracers : (f + 1) * tracers, at] = high
             stacked[half + f * tracers : half + (f + 1) * tracers, at] = low
-        rim_level(j, rim, index, weights, e_out)
         if (j + 1) % (groups // 2) == 0:
             part = pl.ds((j + 1 - groups // 2) * LANES, groups // 2 * LANES)
             term = jnp.dot(stacked[:, part], q[part, :], preferred_element_type=F32)
@@ -191,9 +147,35 @@
     slots = slots[:half] + slots[half:]
     r_out[...] = slots[:rows] * live[...]
     w_out[...] = slots[rows:] * live[...]
-    if not first:
-        for level in range(groups):
+
+
+def rim_first(ring_a, ring_b, index, weights, e_out, rim, *, axes):
+    flow, cross = axes
+
+    @pl.when(lax.axis_index(flow) == 0)
+    def _():
+        rim_sources(ring_a, ring_b, rim, cross)
+        for level in range(index.shape[1] // LANES):
+            rim_level(level, rim, index, weights, e_out)
+
+
+def rim_rest(ring_a, ring_b, index, weights, order, _, e_out, s_out, own, qt, rim, *, axes):
+    flow, cross = axes
+    cells = qt.shape[0]
+    for level in range(cells // LANES):
+        at = slice(level * LANES, (level + 1) * LANES)
+        spread = jnp.broadcast_to(order[:, at].astype(F32), (LANES, LANES)).T
+        for j in range(cells // LANES):
+            hit = spread == (iota((LANES, LANES), 1) + j * LANES).astype(F32)
+            qt[at, j * LANES : (j + 1) * LANES] = jnp.where(hit, 1.0, 0.0).astype(BF16)
+
+    @pl.when(lax.axis_index(flow) > 0)
+    def _():
+        rim_sources(ring_a, ring_b, rim, cross)
+        for level in range(cells // LANES):
+            rim_level(level, rim, index, weights, e_out)
             inflow_weights(level, index, weights, s_out)
+            own_weights(level, index, weights, own)
 
 
 def gathered(source, lane):
@@ -262,8 +244,31 @@
     s_out[:, slice(s_out.shape[1] // 2 + at.start, s_out.shape[1] // 2 + at.stop)] = low
 
 
+def older_rows(level):
+    return sum(max(v - LAG + 1, 0) for v in range(level)) * LANES
+
+
+def own_weights(level, index, weights, own):
+    depth = (level - LAG + 1) * LANES
+    if depth <= 0:
+        return
+    at = slice(level * LANES, (level + 1) * LANES)
+    source = iota((depth, LANES), 0) + 3 * LANES
+    total = None
+    for face in range(index.shape[0]):
+        if inflow_only(face, level):
+            continue
+        hit = index[face : face + 1, at] == source
+        term = jnp.where(hit, weights[face : face + 1, at], 0.0)
+        total = term if total is None else total + term
+    high, low = split(total)
+    start = older_rows(level)
+    own[start : start + depth, :LANES] = high
+    own[start : start + depth, LANES:] = low
+
+
 def sweep(
-    inflow, live, r, w, index, weights, s, e, qt, back, traces_out, pool, ends, stacked, face_dofs
+    inflow, live, r, w, index, weights, s, own, e, traces_out, pool, ends, narrow, stacked, face_dofs
 ):
     faces, cells = index.shape
     levels = cells // LANES
@@ -291,10 +296,24 @@
         else:
             half = slice(level % 2 * LANES, (level % 2 + 1) * LANES)
             sums = [given[rows_of(i), half] for i in range(count)]
+        oldest = 0
+        if own is not None and level >= LAG:
+            oldest = level - LAG + 1
+            start = older_rows(level)
+            got = jnp.dot(
+                narrow[:, : oldest * LANES],
+                own[start : start + oldest * LANES, :],
+                preferred_element_type=F32,
+            )
+            got = got[:rows, :LANES] + (got[rows:, :LANES] + got[:rows, LANES:])
+            sums = [sums[i] + got[rows_of(i), :] for i in range(count)]
         for face in range(faces):
             if inflow_only(face, level) or level == 0:
                 continue
-            sources = [(3 + v, lambda i, v=v: pool[v, rows_of(i), :]) for v in range(level)]
+            sources = [
+                (3 + v, lambda i, v=v: pool[v, rows_of(i), :])
+                for v in range(oldest, level)
+            ]
             values = face_values(face, level, sources, index, count)
             weight = jnp.broadcast_to(weights[face : face + 1, at], (SUB, LANES))
             for i in range(count):
@@ -319,11 +338,10 @@
                     pool[level, rows_of(i), :] = value
                 else:
                     traces_out[rows_of(i), :] = value
-        if back is not None and level % 2 == 1:
-            both = slice((level - 1) * LANES, (level + 1) * LANES)
-            moved = jnp.dot(stacked[:, both], qt[both, :], preferred_element_type=F32)
-            moved = moved[:rows] + moved[rows:]
-            back[...] = moved if level == 1 else back[...] + moved
+        if own is not None and level < levels - LAG:
+            high, low = split(pool[level])
+            narrow[:rows, at] = high
+            narrow[rows:, at] = low
 
 
 def local_group(j, live, inv, rhs, q, p_out, wide):
@@ -337,7 +355,7 @@
     )[:1]
     for a in range(block):
         wide[a * block : (a + 1) * block, :] = inv[a, :, at].astype(F32) * mask
-    step = 4
+    step = block // 2
 
     def some(part, carry):
         sums = [None] * step
@@ -357,10 +375,11 @@
 def local_plan(flows, groups):
     plan = []
     for f in range(flows):
-        steps = [("turn", m) for m in range(f) if (f, m) != (1, 0)]
-        steps += [("window", m) for m in range(max(f, min(1, flows - 2)), flows - 1)]
-        steps = steps or [("final", flows - 1)]
-        ends = [-(-k * groups // len(steps)) for k in range(len(steps) + 1)]
+        turns = [("turn", m) for m in range(f if f > 2 else f - 1)]
+        late = [("window", m) for m in range(max(f, min(1, flows - 2)), flows - 1)]
+        steps = turns + late or [("final", flows - 1)]
+        shares = [1] * len(turns) + [2] * len(late) or [1]
+        ends = [-(-sum(shares[:k]) * groups // sum(shares)) for k in range(len(steps) + 1)]
         plan.append({step: (ends[k], ends[k + 1]) for k, step in enumerate(steps)})
     return plan
 
@@ -381,20 +400,13 @@
     )
 
 
-def turn(*refs, moment, flow, face_dofs, fused):
+def turn(*refs, moment, flow, face_dofs):
     refs = list(refs)
     inflow = refs.pop(0) if moment > 0 else None
     live, r, w, index, weights, e = refs[:6]
-    refs = refs[6:]
-    s = qt = ends = back = None
-    if moment > 0:
-        s, qt = refs[:2]
-        refs = refs[2:]
-    if fused:
-        back, traces_out, stacked, pool, ends = refs
-    else:
-        inv, rhs, q, _, _, p_out, stacked, traces_out, pool, wide = refs[:10]
-        ends = refs[10] if moment > 0 else None
+    s, own = (refs.pop(6), refs.pop(6)) if moment > 0 else (None, None)
+    inv, rhs, q, _, _, p_out, stacked, traces_out, pool, wide = refs[6:16]
+    ends, narrow = refs[16:] if moment > 0 else (None, None)
 
     @pl.when(lax.axis_index(flow) == moment)
     def _():
@@ -406,67 +418,76 @@
             index,
             weights,
             s,
+            own,
             e,
-            qt,
-            back,
             traces_out,
             pool,
             ends,
+            narrow,
             stacked,
             face_dofs,
         )
 
-    if not fused:
-        planned_groups(("turn", moment), flow, live, inv, rhs, q, p_out, wide)
+    planned_groups(("turn", moment), flow, live, inv, rhs, q, p_out, wide)
 
 
 def window(live, inv, rhs, q, _, p_out, wide, *, moment, flow):
     planned_groups(("window", moment), flow, live, inv, rhs, q, p_out, wide)
 
 
-def move_back(carried, qt, back):
-    moved = jnp.dot(carried[...], qt[...], preferred_element_type=F32)
-    rows = back.shape[0]
-    back[...] = moved[:rows] + moved[rows:]
-
-
-def early(live, inv, rhs, q, carried, qt, il, _, p, out, wide, back, done, sem, *, moment, flow):
+def early(live, inv, rhs, q, carried, qt, il, _, p, out, wide, done, sem, *, moment, flow):
     planned_groups(("window", moment), flow, live, inv, rhs, q, p, wide)
 
     @pl.when(lax.axis_index(flow) <= moment)
     def _():
-        move_back(carried, qt, back)
-        write_solution(back, p, il, out, done, sem)
-
-
-def final(live, inv, rhs, q, back, qt, il, _, out_in, p, out, wide, moved, done, sem, *, flow, fused):
+        write_solution(carried, qt, p, il, out, done, sem)
+
+
+def final(live, inv, rhs, q, carried, qt, il, _, out_in, p, out, wide, done, sem, *, flow):
     last = lax.axis_size(flow) - 1
     planned_groups(("final", last), flow, live, inv, rhs, q, p, wide)
 
     @pl.when(lax.axis_index(flow) == last)
     def _():
-        if not fused:
-            move_back(back, qt, moved)
-        write_solution(back if fused else moved, p, il, out, done, sem)
-
-
-def write_solution(back, p, il, out, done, sem):
+        write_solution(carried, qt, p, il, out, done, sem)
+
+
+def write_solution(carried, qt, p, il, out, done, sem):
     block, tracers, cells = p.shape
-    face_dofs = back.shape[0] // tracers
-    copies = []
-    for a in range(block):
-        for j in range(cells // LANES):
-            at = pl.ds(j * LANES, LANES)
-            value = p[a, :, at]
-            for g in range(face_dofs):
-                scale = il[g * block + a : g * block + a + 1, at]
-                value = value + scale * back[g * tracers : (g + 1) * tracers, at]
-            done[a, :, at] = value
-        copy = pltpu.make_async_copy(done.at[a], out.at[a], sem.at[a])
-        copy.start()
-        copies.append(copy)
-    for copy in copies:
-        copy.wait()
+    rows = carried.shape[0] // 2
+    face_dofs = rows // tracers
+    width = 2 * LANES
+    parts = cells // width
+
+    def copy_of(part):
+        at = pl.ds(pl.multiple_of(part * width, width), width)
+        return pltpu.make_async_copy(done.at[:, :, at], out.at[:, :, at], sem.at[part])
+
+    def moved_to(part):
+        cols = pl.ds(pl.multiple_of(part * width, width), width)
+        back = jnp.dot(carried[...], qt[:, cols], preferred_element_type=F32)
+        return back[:rows] + back[rows:]
+
+    def write(part, moved):
+        for k in range(2):
+            at = pl.ds(pl.multiple_of(part * width + k * LANES, LANES), LANES)
+            half = slice(k * LANES, (k + 1) * LANES)
+            for a in range(block):
+                value = p[a, :, at]
+                for g in range(face_dofs):
+                    scale = il[g * block + a : g * block + a + 1, at]
+                    value = value + scale * moved[g * tracers : (g + 1) * tracers, half]
+                done[a, :, at] = value
+        copy_of(part).start()
+
+    def one(part, moved):
+        following = moved_to(part + 1)
+        write(part, moved)
+        return following
+
+    write(parts - 1, lax.fori_loop(0, parts - 1, one, moved_to(0)))
+    for part in range(parts):
+        copy_of(part).wait()
 
 
 def swaps(flows, columns, partner):
@@ -483,9 +504,7 @@
 def rim_partner(first, columns):
     def partner(f, c):
         other = c + 1 if c % 2 == first else c - 1
-        if columns % 2 == 0:
-            other %= columns
-        return f, other
+        return (f, other) if 0 <= other < columns else (f ^ 1, c)
 
     return partner
 
@@ -557,28 +576,8 @@
         in_hbm(lift_map.T),
     )
 
-    made_shapes = [
-        pltpu.VMEM((rows, cells), F32),
-        pltpu.VMEM((WROWS, cells), F32),
-        pltpu.VMEM((rows, cells), F32),
-        pltpu.VMEM((LANES, 2 * cells), BF16),
-    ]
-    local_scratch = [
-        pltpu.VMEM((2 * (rows + WROWS), cells), BF16),
-        pltpu.VMEM((2, rows, LANES), F32),
-    ]
-    local_given = [in_vmem(ring_a), in_vmem(ring_b), ti, mix, rhs, q, live, index, weights]
-    r, w, e, s = pl.pallas_call(
-        functools.partial(local_first, axes=axes),
-        out_shape=made_shapes,
-        in_specs=[VM] * 9,
-        out_specs=[VM] * 4,
-        scratch_shapes=local_scratch,
-        compiler_params=params(12),
-        name="local_first",
-    )(*local_given)
-
-    back_shape = pltpu.VMEM((rows, cells), F32)
+    e_shape = pltpu.VMEM((rows, cells), F32)
+    rim_shape = pltpu.VMEM((2, rows, LANES), F32)
     p_shape = pltpu.VMEM((block, tracers, cells), F32)
     halves = pltpu.VMEM((2 * rows, cells), BF16)
     sent = pltpu.VMEM((rows, LANES), F32)
@@ -586,52 +585,65 @@
     wide = pltpu.VMEM((block * block, LANES), F32)
     ends = pltpu.VMEM((2 * rows, LANES), BF16)
     out_shape = pltpu.HBM((block, tracers, cells), F32)
-    out_scratch = [p_shape, pltpu.SemaphoreType.DMA((block,))]
-    qt = received = out = back = None
+    out_scratch = [wide, p_shape, pltpu.SemaphoreType.DMA((cells // (2 * LANES),))]
+
+    r, w = pl.pallas_call(
+        products,
+        out_shape=[pltpu.VMEM((rows, cells), F32), pltpu.VMEM((WROWS, cells), F32)],
+        in_specs=[VM] * 5,
+        out_specs=[VM] * 2,
+        scratch_shapes=[pltpu.VMEM((2 * (rows + WROWS), cells), BF16)],
+        compiler_params=params(8),
+        name="products",
+    )(ti, mix, rhs, q, live)
+    rim_given = [in_vmem(ring_a), in_vmem(ring_b), index, weights]
+    e = pl.pallas_call(
+        functools.partial(rim_first, axes=axes),
+        out_shape=e_shape,
+        in_specs=[VM] * 4,
+        out_specs=VM,
+        scratch_shapes=[rim_shape],
+        compiler_params=params(4),
+        name="rim_first",
+    )(*rim_given)
+
+    s = own = qt = received = out = None
     for moment in range(flows):
         last = moment == flows - 1
-        fused = last and moment > 0
         given = [] if moment == 0 else [in_vmem(received)]
-        given += [live, r, w, index, weights, e] + ([] if moment == 0 else [s, qt])
-        more = [] if moment == 0 else [ends]
-        run = functools.partial(
-            turn, moment=moment, flow="flow", face_dofs=face_dofs, fused=fused
-        )
-        if fused:
-            back = pl.pallas_call(
-                run,
-                out_shape=back_shape,
-                in_specs=[VM] * len(given),
-                out_specs=VM,
-                scratch_shapes=[sent, halves, pool, ends],
-                compiler_params=params(4),
-                name=f"turn{moment}",
-            )(*given)
-            break
+        given += [live, r, w, index, weights, e] + ([] if moment == 0 else [s, own])
         given += [inv, rhs, q, p, carried]
-        p, carried, traces = pl.pallas_call(
-            run,
-            out_shape=[p_shape, halves, sent],
+        made = pl.pallas_call(
+            functools.partial(turn, moment=moment, flow="flow", face_dofs=face_dofs),
+            out_shape=[p_shape, halves] + ([] if last else [sent]),
             in_specs=[VM] * len(given),
-            out_specs=[VM] * 3,
+            out_specs=[VM] * (2 if last else 3),
             input_output_aliases={len(given) - 2: 0, len(given) - 1: 1},
-            scratch_shapes=[pool, wide] + more,
+            scratch_shapes=([sent] if last else [])
+            + [pool, wide]
+            + ([] if moment == 0 else [ends, halves]),
             compiler_params=params(4),
             name=f"turn{moment}",
         )(*given)
+        p, carried = made[:2]
         if not last:
-            received = lax.ppermute(traces, axes, swaps(flows, columns, hop_partner(moment)))
+            received = lax.ppermute(made[2], axes, swaps(flows, columns, hop_partner(moment)))
         if moment == 0:
-            r, w, e, s, qt = pl.pallas_call(
-                functools.partial(local_rest, axes=axes),
-                out_shape=made_shapes + [pltpu.VMEM((cells, cells), BF16)],
-                in_specs=[VM] * 14,
-                out_specs=[VM] * 5,
-                input_output_aliases={10: 0, 11: 1, 12: 2, 13: 3},
-                scratch_shapes=local_scratch,
-                compiler_params=params(12),
-                name="local_rest",
-            )(*local_given, order, r, w, e, s)
+            e, s, own, qt = pl.pallas_call(
+                functools.partial(rim_rest, axes=axes),
+                out_shape=[
+                    e_shape,
+                    pltpu.VMEM((LANES, 2 * cells), BF16),
+                    pltpu.VMEM((max(older_rows(cells // LANES), LANES), 2 * LANES), BF16),
+                    pltpu.VMEM((cells, cells), BF16),
+                ],
+                in_specs=[VM] * 6,
+                out_specs=[VM] * 4,
+                input_output_aliases={5: 0},
+                scratch_shapes=[rim_shape],
+                compiler_params=params(8),
+                name="rim_rest",
+            )(*rim_given, order, e)
         if moment == flows - 2:
             p, out = pl.pallas_call(
                 functools.partial(early, moment=moment, flow="flow"),
@@ -639,7 +651,7 @@
                 in_specs=[VM] * 8,
                 out_specs=[VM, far],
                 input_output_aliases={7: 0},
-                scratch_shapes=[wide, back_shape] + out_scratch,
+                scratch_shapes=out_scratch,
                 compiler_params=params(8),
                 name="early",
             )(live, inv, rhs, q, carried, qt, il, p)
@@ -658,15 +670,15 @@
     if out is None:
         out = jnp.zeros((block, tracers, cells), F32)
     p, out = pl.pallas_call(
-        functools.partial(final, flow="flow", fused=fused),
+        functools.partial(final, flow="flow"),
         out_shape=[p_shape, out_shape],
         in_specs=[VM] * 8 + [far],
         out_specs=[VM, far],
         input_output_aliases={7: 0, 8: 1},
-        scratch_shapes=[wide, back_shape] + out_scratch,
+        scratch_shapes=out_scratch,
         compiler_params=params(8),
         name="final",
-    )(live, inv, rhs, q, back if fused else carried, qt, il, p, out)
+    )(live, inv, rhs, q, carried, qt, il, p, out)
     return out[None, None]
 
 

time: 24.1 us -> 21.5 us (0.89)
  starting transfers between devices: 7.27 us -> 5.32 us
  waiting for transfers between devices: 4.15 us -> 3.22 us
  Pallas kernels: 12.3 us -> 12.7 us
    ppermute x3, starting transfers between devices: 5.66 us -> 3.71 us  [shards(): lax.ppermute(made[2], axes, swaps(flows, columns, hop_partner(moment)))]
    ppermute x1, waiting for transfers between devices: 1.03 us -> 0.01 us  [shards(): lax.ppermute(edges, axes, swaps(flows, columns, rim_partner(1, columns)))]
    pallas_call x7 -> x8, Pallas kernels: 10.5 us -> 10.9 us  [the longest x4 5.35 us: shards(): pl.pallas_call(functools.partial(turn, moment=moment, flow='flow', face_d...]
  transfers between devices with their start and end apart: 5 -> 5, of which waited for: 3 -> 2; matrix products, arithmetic and copies ran while one was open for 0% -> 0% of each run, Pallas kernels for 17% -> 24%
where the time goes in v3:
time: 21.5 us; the launch traced here: 21.3 us
  Pallas kernels  12.7 us (59%)
  starting transfers between devices  5.32 us (25%)
  waiting for transfers between devices  3.22 us (15%)
    pallas_call x4, Pallas kernels, shards(): pl.pallas_call(functools.partial(turn, moment=moment, flow='flow', face_d...  5.35 us
    ppermute x3, starting transfers between devices, shards(): lax.ppermute(made[2], axes, swaps(flows, columns, hop_partner(moment)))  3.71 us
    ppermute x3, waiting for transfers between devices, shards(): lax.ppermute(made[2], axes, swaps(flows, columns, hop_partner(moment)))  3.22 us
    pallas_call x1, Pallas kernels, shards(): pl.pallas_call(functools.partial(final, flow='flow'), out_shape=[p_shape,...  2.28 us
    pallas_call x1, Pallas kernels, shards(): pl.pallas_call(functools.partial(rim_rest, axes=axes), out_shape=[e_shape...  2.1 us
    pallas_call x1, Pallas kernels, shards(): pl.pallas_call(load, out_shape=(pltpu.VMEM((face_dofs * block, cells), F3...  1.69 us
    ppermute x1, starting transfers between devices, shards(): lax.ppermute(edges, axes, swaps(flows, columns, rim_partner(0, columns)))  1.6 us
    pallas_call x1, Pallas kernels, shards(): pl.pallas_call(products, out_shape=[pltpu.VMEM((rows, cells), F32), pltpu...  1.19 us
  transfers between devices with their start and end apart: 5, of which 2 were waited for; matrix products, arithmetic and copies ran while one was open for 0% of the time, Pallas kernels for 24%

profile of v3, /device:TPU:26, one launch (start us, length us, event | category | flops | bytes accessed | tf_op | source)
XLA Modules:
  0.0 21.3 jit_solution(13876502749547833390)
XLA Ops:
  0.0 0.0 collective-permute-start.1
  0.0 1.6 %collective-permute-start = (f32[2,96,128]{2,1,0:T(8,128)}, f32[2,96,128]{2,1,0:T(8,128)S(1)}, u32[]{:S(2)}, u32[]{:S(2)}) collective-permute-start(f32[2,96,128]{2,1,0:T(8,128)} %bitcast.17), channel_id=1, source_target_pairs={{0,1},{1,0},{2,3},{3,2},{4,5},{5,4},{6,7},{7,6},{8,9},{9,8},{10,11... | collective-permute-start | bytes 294920 | tf_op jit(solution)/shard_map/ppermute | solution.py:537
  1.6 1.7 %load.1 = (f32[48,1024]{1,0:T(8,128)S(1)}, f32[48,1024]{1,0:T(8,128)S(1)}, bf16[32,1024]{1,0:T(8,128)(2,1)S(1)}, bf16[1024,1024]{1,0:T(8,128)(2,1)S(1)}, bf16[16...) custom-call(s32[8]{0:T(128)} %bitcast.15, ...), custom_call_target="tpu_custom_call" | custom-call | tf_op jit(solution)/shard_map/load/pallas_call | solution.py:542
  3.3 1.2 %products.1 = (f32[96,1024]{1,0:T(8,128)S(1)}, f32[16,1024]{1,0:T(8,128)S(1)}) custom-call(f32[48,1024]{1,0:T(8,128)S(1)} %get-tuple-element.41.ti, bf16[32,1024]{1,0:T(8,128)(2,1)S(1)} %get-tuple-element.42.mix, bf16[16,32,1024]{2,1,0:T(8,128)(2,1)S(1)} %get-tuple-element.39.rhs.refs_7_.refs_10_, ...), custom_call_target="tpu_custom_call" | custom-call | tf_op jit(solution)/shard_map/products/pallas_call | solution.py:590
  4.5 0.0 collective-permute-done.1.ring_b
  4.5 0.0 collective-permute-done.ring_a
  4.5 1.6 %turn0.1 = (f32[16,32,1024]{2,1,0:T(8,128)S(1)}, bf16[192,1024]{1,0:T(8,128)(2,1)S(1)}, f32[96,128]{1,0:T(8,128)S(1)}) custom-call(f32[1,1024]{1,0:T(1,128)S(1)} %get-tuple-element.37.live.refs_0_.refs_1_, f32[96,1024]{1,0:T(8,128)S(1)} %get-tuple-element.43.refs_1_.refs_2_, ...), custom_call_target="tpu_custom_call", output_to_operand_aliasing={{0}: (9, {}), {1}: (10, {})} | custom-call | tf_op jit(solution)/shard_map/turn0/pallas_call | solution.py:616
  6.1 1.5 %collective-permute-start.2 = (f32[96,128]{1,0:T(8,128)S(1)}, f32[96,128]{1,0:T(8,128)S(1)}, u32[]{:S(2)}, u32[]{:S(2)}) collective-permute-start(f32[96,128]{1,0:T(8,128)S(1)} %get-tuple-element.49), channel_id=1, source_target_pairs={{0,8},{1,9},{2,10},{3,11},{4,12},{5,13},{6,14},{7,15},{8,0},{9,1},... | collective-permute-start | bytes 147464 | tf_op jit(solution)/shard_map/ppermute | solution.py:630
  7.6 2.1 %rim_rest.1 = (f32[96,1024]{1,0:T(8,128)S(1)}, bf16[128,2048]{1,0:T(8,128)(2,1)S(1)}, bf16[1920,256]{1,0:T(8,128)(2,1)S(1)}, bf16[1024,1024]{1,0:T(8,128)(2,1)S(1)}) custom-call(f32[2,96,128]{2,1,0:T(8,128)S(1)} %collective-permute-done.ring_a, f32[2,96,128]{2,1,0:T(8,128)S(1)} %collective-permute-done.1.ring_b, ...), custom_call_target="tpu_custom_call", output_to_operand_aliasing={{0}: (5, {})} | custom-call | tf_op jit(solution)/shard_map/rim_rest/pallas_call | solution.py:632
  9.7 0.0 collective-permute-done.2.refs_0_
  9.7 1.6 %turn1.1 = (f32[16,32,1024]{2,1,0:T(8,128)S(1)}, bf16[192,1024]{1,0:T(8,128)(2,1)S(1)}, f32[96,128]{1,0:T(8,128)S(1)}) custom-call(f32[96,128]{1,0:T(8,128)S(1)} %collective-permute-done.2.refs_0_, f32[1,1024]{1,0:T(1,128)S(1)} %get-tuple-element.37.live.refs_0_.refs_1_, ...), custom_call_target="tpu_custom_call", output_to_operand_aliasing={{0}: (12, {}), {1}: (13, {})} | custom-call | tf_op jit(solution)/shard_map/turn1/pallas_call | solution.py:616
  11.3 0.1 collective-permute-start.3
  11.4 1.2 %collective-permute-done.3.refs_0_ = f32[96,128]{1,0:T(8,128)S(1)} collective-permute-done((f32[96,128]{1,0:T(8,128)S(1)}, f32[96,128]{1,0:T(8,128)S(1)}, u32[]{:S(2)}, u32[]{:S(2)}) %collective-permute-start.3) | collective-permute-done | bytes 49184 | tf_op jit(solution)/shard_map/ppermute | solution.py:630
  12.6 1.0 %turn2.1 = (f32[16,32,1024]{2,1,0:T(8,128)S(1)}, bf16[192,1024]{1,0:T(8,128)(2,1)S(1)}, f32[96,128]{1,0:T(8,128)S(1)}) custom-call(f32[96,128]{1,0:T(8,128)S(1)} %collective-permute-done.3.refs_0_, f32[1,1024]{1,0:T(1,128)S(1)} %get-tuple-element.37.live.refs_0_.refs_1_, ...), custom_call_target="tpu_custom_call", output_to_operand_aliasing={{0}: (12, {}), {1}: (13, {})} | custom-call | tf_op jit(solution)/shard_map/turn2/pallas_call | solution.py:616
  13.7 2.1 %collective-permute-start.4 = (f32[96,128]{1,0:T(8,128)S(1)}, f32[96,128]{1,0:T(8,128)S(1)}, u32[]{:S(2)}, u32[]{:S(2)}) collective-permute-start(f32[96,128]{1,0:T(8,128)S(1)} %get-tuple-element.59), channel_id=1, source_target_pairs={{0,1},{1,0},{2,3},{3,2},{4,5},{5,4},{6,7},{7,6},{8,9},{9,8},{10,11... | collective-permute-start | bytes 147464 | tf_op jit(solution)/shard_map/ppermute | solution.py:630
  15.9 2.0 %collective-permute-done.4.refs_0_ = f32[96,128]{1,0:T(8,128)S(1)} collective-permute-done((f32[96,128]{1,0:T(8,128)S(1)}, f32[96,128]{1,0:T(8,128)S(1)}, u32[]{:S(2)}, u32[]{:S(2)}) %collective-permute-start.4) | collective-permute-done | bytes 49184 | tf_op jit(solution)/shard_map/ppermute | solution.py:630
  17.9 1.2 %turn3.1 = (f32[16,32,1024]{2,1,0:T(8,128)S(1)}, bf16[192,1024]{1,0:T(8,128)(2,1)S(1)}) custom-call(f32[96,128]{1,0:T(8,128)S(1)} %collective-permute-done.4.refs_0_, f32[1,1024]{1,0:T(1,128)S(1)} %get-tuple-element.37.live.refs_0_.refs_1_, f32[96,1024]{1,0:T(8,128)S(1)} %get-tuple-element.43.refs_1_.refs_2_, ...), custom_call_target="tpu_custom_call", output_to_operand_aliasing={{0}: (12, {}), {1}: (13, {})} | custom-call | tf_op jit(solution)/shard_map/turn3/pallas_call | solution.py:616
  19.0 2.3 %final.1 = (f32[16,32,1024]{2,1,0:T(8,128)S(1)}, f32[16,32,1024]{2,1,0:T(8,128)}) custom-call(f32[1,1024]{1,0:T(1,128)S(1)} %get-tuple-element.37.live.refs_0_.refs_1_, bf16[16,16,1024]{2,1,0:T(8,128)(2,1)S(1)} %get-tuple-element.38.refs_6_.refs_9_.inv, ...), custom_call_target="tpu_custom_call", output_to_operand_aliasing={{0}: (7, {}), {1}: (8, {})} | custom-call | tf_op jit(solution)/shard_map/final/pallas_call | solution.py:672
  (3 shorter events, 0.1 us)
Async XLA Ops:
  0.0 4.5 %collective-permute-start.1 = (f32[2,96,128]{2,1,0:T(8,128)}, f32[2,96,128]{2,1,0:T(8,128)S(1)}, u32[]{:S(2)}, u32[]{:S(2)}) collective-permute-start(f32[2,96,128]{2,1,0:T(8,128)} %bitcast.16), channel_id=1, source_target_pairs={{0,8},{1,2},{2,1},{3,4},{4,3},{5,6},{6,5},{7,15},{8,0},{9,10},{10,... | collective-permute-start | bytes 294920 | tf_op jit(solution)/shard_map/ppermute | solution.py:538
  0.0 4.5 %collective-permute-start = (f32[2,96,128]{2,1,0:T(8,128)}, f32[2,96,128]{2,1,0:T(8,128)S(1)}, u32[]{:S(2)}, u32[]{:S(2)}) collective-permute-start(f32[2,96,128]{2,1,0:T(8,128)} %bitcast.17), channel_id=1, source_target_pairs={{0,1},{1,0},{2,3},{3,2},{4,5},{5,4},{6,7},{7,6},{8,9},{9,8},{10,11... | collective-permute-start | bytes 294920 | tf_op jit(solution)/shard_map/ppermute | solution.py:537
  6.1 3.6 %collective-permute-start.2 = (f32[96,128]{1,0:T(8,128)S(1)}, f32[96,128]{1,0:T(8,128)S(1)}, u32[]{:S(2)}, u32[]{:S(2)}) collective-permute-start(f32[96,128]{1,0:T(8,128)S(1)} %get-tuple-element.49), channel_id=1, source_target_pairs={{0,8},{1,9},{2,10},{3,11},{4,12},{5,13},{6,14},{7,15},{8,0},{9,1},... | collective-permute-start | bytes 147464 | tf_op jit(solution)/shard_map/ppermute | solution.py:630
  11.3 1.3 %collective-permute-start.3 = (f32[96,128]{1,0:T(8,128)S(1)}, f32[96,128]{1,0:T(8,128)S(1)}, u32[]{:S(2)}, u32[]{:S(2)}) collective-permute-start(f32[96,128]{1,0:T(8,128)S(1)} %get-tuple-element.56), channel_id=1, source_target_pairs={{0,1},{1,0},{2,3},{3,2},{4,5},{5,4},{6,7},{7,6},{8,16},{9,17},{10,... | collective-permute-start | bytes 147464 | tf_op jit(solution)/shard_map/ppermute | solution.py:630
  13.7 4.2 %collective-permute-start.4 = (f32[96,128]{1,0:T(8,128)S(1)}, f32[96,128]{1,0:T(8,128)S(1)}, u32[]{:S(2)}, u32[]{:S(2)}) collective-permute-start(f32[96,128]{1,0:T(8,128)S(1)} %get-tuple-element.59), channel_id=1, source_target_pairs={{0,1},{1,0},{2,3},{3,2},{4,5},{5,4},{6,7},{7,6},{8,9},{9,8},{10,11... | collective-permute-start | bytes 147464 | tf_op jit(solution)/shard_map/ppermute | solution.py:630

commit v4 on v3

--- a/solution.py
+++ b/solution.py
@@ -98,9 +98,14 @@
     for copy in copies[:3]:
         copy.wait()
     high, low = split(coefficients(trace_map[...], lift_map[...], block))
-    for j in range(cells // LANES):
-        hit = iota((LANES, cells), 0) + j * LANES == order[...]
-        q[j * LANES : (j + 1) * LANES, :] = jnp.where(hit, 1.0, 0.0).astype(BF16)
+    groups = cells // LANES
+
+    def mark(first, end):
+        for j in range(first, end):
+            hit = iota((LANES, cells), 0) + j * LANES == order[...]
+            q[j * LANES : (j + 1) * LANES, :] = jnp.where(hit, 1.0, 0.0).astype(BF16)
+
+    mark(0, groups)
     copies[7].wait()
     for level in range(cells // LANES):
         here = iota((1, LANES), 1) < counts[level]
@@ -119,7 +124,7 @@
         copy.wait()
 
 
-def products(ti, mix, rhs, q, live, r_out, w_out, stacked):
+def products(ti, mix, rhs, q, live, index, weights, r_out, w_out, own, stacked):
     block, tracers, cells = rhs.shape
     rows = r_out.shape[0]
     faces = rows // tracers
@@ -140,10 +145,12 @@
             high, low = split(sums[f])
             stacked[f * tracers : (f + 1) * tracers, at] = high
             stacked[half + f * tracers : half + (f + 1) * tracers, at] = low
-        if (j + 1) % (groups // 2) == 0:
-            part = pl.ds((j + 1 - groups // 2) * LANES, groups // 2 * LANES)
+        if (j + 1) % (groups // 4) == 0:
+            part = pl.ds((j + 1 - groups // 4) * LANES, groups // 4 * LANES)
             term = jnp.dot(stacked[:, part], q[part, :], preferred_element_type=F32)
             slots = term if slots is None else slots + term
+    for level in range(groups):
+        own_weights(level, index, weights, own)
     slots = slots[:half] + slots[half:]
     r_out[...] = slots[:rows] * live[...]
     w_out[...] = slots[rows:] * live[...]
@@ -159,8 +166,7 @@
             rim_level(level, rim, index, weights, e_out)
 
 
-def rim_rest(ring_a, ring_b, index, weights, order, _, e_out, s_out, own, qt, rim, *, axes):
-    flow, cross = axes
+def storage_order(order, live, qt, mask):
     cells = qt.shape[0]
     for level in range(cells // LANES):
         at = slice(level * LANES, (level + 1) * LANES)
@@ -168,14 +174,31 @@
         for j in range(cells // LANES):
             hit = spread == (iota((LANES, LANES), 1) + j * LANES).astype(F32)
             qt[at, j * LANES : (j + 1) * LANES] = jnp.where(hit, 1.0, 0.0).astype(BF16)
+    rows = jnp.broadcast_to(live[...], (WROWS, cells)).astype(BF16)
+    mask[...] = jnp.dot(rows, qt[...], preferred_element_type=F32)[:1]
+
+
+def order_second(order, live, qt_in, mask_in, qt, mask, *, flow):
+    @pl.when(lax.axis_index(flow) == 1)
+    def _():
+        storage_order(order, live, qt, mask)
+
+
+def rim_rest(
+    ring_a, ring_b, index, weights, order, live, _, e_out, s_out, qt, mask, rim, *, axes
+):
+    flow, cross = axes
+
+    @pl.when(lax.axis_index(flow) != 1)
+    def _():
+        storage_order(order, live, qt, mask)
 
     @pl.when(lax.axis_index(flow) > 0)
     def _():
         rim_sources(ring_a, ring_b, rim, cross)
-        for level in range(cells // LANES):
+        for level in range(index.shape[1] // LANES):
             rim_level(level, rim, index, weights, e_out)
             inflow_weights(level, index, weights, s_out)
-            own_weights(level, index, weights, own)
 
 
 def gathered(source, lane):
@@ -344,17 +367,12 @@
             narrow[rows:, at] = low
 
 
-def local_group(j, live, inv, rhs, q, p_out, wide):
+def local_group(j, mask, inv, rhs, p_out, wide):
     block = inv.shape[0]
-    cells = rhs.shape[2]
     start = pl.multiple_of(j * LANES, LANES)
     at = pl.ds(start, LANES)
-    rows = jnp.broadcast_to(live[...], (WROWS, cells)).astype(BF16)
-    mask = lax.dot_general(
-        rows, q[at, :], (((1,), (1,)), ((), ())), preferred_element_type=F32
-    )[:1]
     for a in range(block):
-        wide[a * block : (a + 1) * block, :] = inv[a, :, at].astype(F32) * mask
+        wide[a * block : (a + 1) * block, :] = inv[a, :, at].astype(F32) * mask[:, at]
     step = block // 2
 
     def some(part, carry):
@@ -375,16 +393,16 @@
 def local_plan(flows, groups):
     plan = []
     for f in range(flows):
-        turns = [("turn", m) for m in range(f if f > 2 else f - 1)]
+        turns = [("turn", m) for m in range(1, f if f > 2 else f - 1)]
         late = [("window", m) for m in range(max(f, min(1, flows - 2)), flows - 1)]
         steps = turns + late or [("final", flows - 1)]
-        shares = [1] * len(turns) + [2] * len(late) or [1]
+        shares = [1] * len(turns) + [3] * len(late) or [1]
         ends = [-(-sum(shares[:k]) * groups // sum(shares)) for k in range(len(steps) + 1)]
         plan.append({step: (ends[k], ends[k + 1]) for k, step in enumerate(steps)})
     return plan
 
 
-def planned_groups(step, flow, live, inv, rhs, q, p_out, wide):
+def planned_groups(step, flow, mask, inv, rhs, p_out, wide):
     flows = lax.axis_size(flow)
     plan = local_plan(flows, rhs.shape[2] // LANES)
     if not any(step in own for own in plan):
@@ -396,17 +414,17 @@
         first = jnp.where(position == f, low, first)
         end = jnp.where(position == f, high, end)
     lax.fori_loop(
-        first, end, lambda j, c: (local_group(j, live, inv, rhs, q, p_out, wide), c)[1], 0
+        first, end, lambda j, c: (local_group(j, mask, inv, rhs, p_out, wide), c)[1], 0
     )
 
 
 def turn(*refs, moment, flow, face_dofs):
     refs = list(refs)
     inflow = refs.pop(0) if moment > 0 else None
-    live, r, w, index, weights, e = refs[:6]
-    s, own = (refs.pop(6), refs.pop(6)) if moment > 0 else (None, None)
-    inv, rhs, q, _, _, p_out, stacked, traces_out, pool, wide = refs[6:16]
-    ends, narrow = refs[16:] if moment > 0 else (None, None)
+    live, r, w, index, weights, e, own = refs[:7]
+    s, mask = (refs.pop(7), refs.pop(7)) if moment > 0 else (None, None)
+    inv, rhs, _, _, p_out, stacked, traces_out, pool, wide, narrow = refs[7:17]
+    ends = refs[17] if moment > 0 else None
 
     @pl.when(lax.axis_index(flow) == moment)
     def _():
@@ -428,24 +446,24 @@
             face_dofs,
         )
 
-    planned_groups(("turn", moment), flow, live, inv, rhs, q, p_out, wide)
-
-
-def window(live, inv, rhs, q, _, p_out, wide, *, moment, flow):
-    planned_groups(("window", moment), flow, live, inv, rhs, q, p_out, wide)
-
-
-def early(live, inv, rhs, q, carried, qt, il, _, p, out, wide, done, sem, *, moment, flow):
-    planned_groups(("window", moment), flow, live, inv, rhs, q, p, wide)
+    planned_groups(("turn", moment), flow, mask, inv, rhs, p_out, wide)
+
+
+def window(mask, inv, rhs, _, p_out, wide, *, moment, flow):
+    planned_groups(("window", moment), flow, mask, inv, rhs, p_out, wide)
+
+
+def early(mask, inv, rhs, carried, qt, il, _, p, out, wide, done, sem, *, moment, flow):
+    planned_groups(("window", moment), flow, mask, inv, rhs, p, wide)
 
     @pl.when(lax.axis_index(flow) <= moment)
     def _():
         write_solution(carried, qt, p, il, out, done, sem)
 
 
-def final(live, inv, rhs, q, carried, qt, il, _, out_in, p, out, wide, done, sem, *, flow):
+def final(mask, inv, rhs, carried, qt, il, _, out_in, p, out, wide, done, sem, *, flow):
     last = lax.axis_size(flow) - 1
-    planned_groups(("final", last), flow, live, inv, rhs, q, p, wide)
+    planned_groups(("final", last), flow, mask, inv, rhs, p, wide)
 
     @pl.when(lax.axis_index(flow) == last)
     def _():
@@ -587,15 +605,19 @@
     out_shape = pltpu.HBM((block, tracers, cells), F32)
     out_scratch = [wide, p_shape, pltpu.SemaphoreType.DMA((cells // (2 * LANES),))]
 
-    r, w = pl.pallas_call(
+    r, w, own = pl.pallas_call(
         products,
-        out_shape=[pltpu.VMEM((rows, cells), F32), pltpu.VMEM((WROWS, cells), F32)],
-        in_specs=[VM] * 5,
-        out_specs=[VM] * 2,
+        out_shape=[
+            pltpu.VMEM((rows, cells), F32),
+            pltpu.VMEM((WROWS, cells), F32),
+            pltpu.VMEM((max(older_rows(cells // LANES), LANES), 2 * LANES), BF16),
+        ],
+        in_specs=[VM] * 7,
+        out_specs=[VM] * 3,
         scratch_shapes=[pltpu.VMEM((2 * (rows + WROWS), cells), BF16)],
         compiler_params=params(8),
         name="products",
-    )(ti, mix, rhs, q, live)
+    )(ti, mix, rhs, q, live, index, weights)
     rim_given = [in_vmem(ring_a), in_vmem(ring_b), index, weights]
     e = pl.pallas_call(
         functools.partial(rim_first, axes=axes),
@@ -607,12 +629,12 @@
         name="rim_first",
     )(*rim_given)
 
-    s = own = qt = received = out = None
+    s = qt = mask = received = out = None
     for moment in range(flows):
         last = moment == flows - 1
         given = [] if moment == 0 else [in_vmem(received)]
-        given += [live, r, w, index, weights, e] + ([] if moment == 0 else [s, own])
-        given += [inv, rhs, q, p, carried]
+        given += [live, r, w, index, weights, e, own] + ([] if moment == 0 else [s, mask])
+        given += [inv, rhs, p, carried]
         made = pl.pallas_call(
             functools.partial(turn, moment=moment, flow="flow", face_dofs=face_dofs),
             out_shape=[p_shape, halves] + ([] if last else [sent]),
@@ -620,8 +642,8 @@
             out_specs=[VM] * (2 if last else 3),
             input_output_aliases={len(given) - 2: 0, len(given) - 1: 1},
             scratch_shapes=([sent] if last else [])
-            + [pool, wide]
-            + ([] if moment == 0 else [ends, halves]),
+            + [pool, wide, halves]
+            + ([] if moment == 0 else [ends]),
             compiler_params=params(4),
             name=f"turn{moment}",
         )(*given)
@@ -629,56 +651,69 @@
         if not last:
             received = lax.ppermute(made[2], axes, swaps(flows, columns, hop_partner(moment)))
         if moment == 0:
-            e, s, own, qt = pl.pallas_call(
+            e, s, qt, mask = pl.pallas_call(
                 functools.partial(rim_rest, axes=axes),
                 out_shape=[
                     e_shape,
                     pltpu.VMEM((LANES, 2 * cells), BF16),
-                    pltpu.VMEM((max(older_rows(cells // LANES), LANES), 2 * LANES), BF16),
                     pltpu.VMEM((cells, cells), BF16),
+                    pltpu.VMEM((1, cells), F32),
                 ],
-                in_specs=[VM] * 6,
+                in_specs=[VM] * 7,
                 out_specs=[VM] * 4,
-                input_output_aliases={5: 0},
+                input_output_aliases={6: 0},
                 scratch_shapes=[rim_shape],
                 compiler_params=params(8),
                 name="rim_rest",
-            )(*rim_given, order, e)
+            )(*rim_given, order, live, e)
+        if moment == 1:
+            qt, mask = pl.pallas_call(
+                functools.partial(order_second, flow="flow"),
+                out_shape=[
+                    pltpu.VMEM((cells, cells), BF16),
+                    pltpu.VMEM((1, cells), F32),
+                ],
+                in_specs=[VM] * 4,
+                out_specs=[VM] * 2,
+                input_output_aliases={2: 0, 3: 1},
+                compiler_params=params(4),
+                name="order_second",
+            )(order, live, qt, mask)
         if moment == flows - 2:
             p, out = pl.pallas_call(
                 functools.partial(early, moment=moment, flow="flow"),
                 out_shape=[p_shape, out_shape],
-                in_specs=[VM] * 8,
+                in_specs=[VM] * 7,
                 out_specs=[VM, far],
-                input_output_aliases={7: 0},
+                input_output_aliases={6: 0},
                 scratch_shapes=out_scratch,
                 compiler_params=params(8),
                 name="early",
-            )(live, inv, rhs, q, carried, qt, il, p)
+            )(mask, inv, rhs, carried, qt, il, p)
         elif 0 < moment < flows - 2:
             p = pl.pallas_call(
                 functools.partial(window, moment=moment, flow="flow"),
                 out_shape=p_shape,
-                in_specs=[VM] * 5,
+                in_specs=[VM] * 4,
                 out_specs=VM,
-                input_output_aliases={4: 0},
+                input_output_aliases={3: 0},
                 scratch_shapes=[wide],
                 compiler_params=params(4),
                 name=f"window{moment}",
-            )(live, inv, rhs, q, p)
+            )(mask, inv, rhs, p)
 
     if out is None:
         out = jnp.zeros((block, tracers, cells), F32)
     p, out = pl.pallas_call(
         functools.partial(final, flow="flow"),
         out_shape=[p_shape, out_shape],
-        in_specs=[VM] * 8 + [far],
+        in_specs=[VM] * 7 + [far],
         out_specs=[VM, far],
-        input_output_aliases={7: 0, 8: 1},
+        input_output_aliases={6: 0, 7: 1},
         scratch_shapes=out_scratch,
         compiler_params=params(8),
         name="final",
-    )(live, inv, rhs, q, carried, qt, il, p, out)
+    )(mask, inv, rhs, carried, qt, il, p, out)
     return out[None, None]
 
 

time: 21.5 us -> 20.8 us (0.967)
  Pallas kernels: 12.7 us -> 11.5 us
  starting transfers between devices: 5.32 us -> 5.69 us
    pallas_call x4, Pallas kernels: 5.35 us -> 3.96 us  [shards(): pl.pallas_call(functools.partial(turn, moment=moment, flow='flow', face_d...]
    pallas_call x1, Pallas kernels: 1.19 us -> 1.65 us  [shards(): pl.pallas_call(products, out_shape=[pltpu.VMEM((rows, cells), F32), pltpu...]
    ppermute x3, starting transfers between devices: 3.71 us -> 4.08 us  [shards(): lax.ppermute(made[2], axes, swaps(flows, columns, hop_partner(moment)))]
    pallas_call x1, Pallas kernels: 2.1 us -> 1.84 us  [shards(): pl.pallas_call(functools.partial(rim_rest, axes=axes), out_shape=[e_shape...]
  transfers between devices with their start and end apart: 5 -> 5, of which waited for: 2 -> 2; matrix products, arithmetic and copies ran while one was open for 0% -> 0% of each run, Pallas kernels for 24% -> 26%
where the time goes in v4:
time: 20.8 us; the launch traced here: 20.5 us
  Pallas kernels  11.5 us (55%)
  starting transfers between devices  5.69 us (27%)
  waiting for transfers between devices  3.2 us (15%)
    ppermute x3, starting transfers between devices, shards(): lax.ppermute(made[2], axes, swaps(flows, columns, hop_partner(moment)))  4.08 us
    pallas_call x4, Pallas kernels, shards(): pl.pallas_call(functools.partial(turn, moment=moment, flow='flow', face_d...  3.96 us
    ppermute x3, waiting for transfers between devices, shards(): lax.ppermute(made[2], axes, swaps(flows, columns, hop_partner(moment)))  3.19 us
    pallas_call x1, Pallas kernels, shards(): pl.pallas_call(functools.partial(final, flow='flow'), out_shape=[p_shape,...  2.28 us
    pallas_call x1, Pallas kernels, shards(): pl.pallas_call(functools.partial(rim_rest, axes=axes), out_shape=[e_shape...  1.84 us
    pallas_call x1, Pallas kernels, shards(): pl.pallas_call(load, out_shape=(pltpu.VMEM((face_dofs * block, cells), F3...  1.69 us
    pallas_call x1, Pallas kernels, shards(): pl.pallas_call(products, out_shape=[pltpu.VMEM((rows, cells), F32), pltpu...  1.65 us
    ppermute x1, starting transfers between devices, shards(): lax.ppermute(edges, axes, swaps(flows, columns, rim_partner(0, columns)))  1.6 us
  transfers between devices with their start and end apart: 5, of which 2 were waited for; matrix products, arithmetic and copies ran while one was open for 0% of the time, Pallas kernels for 26%

profile of v4, /device:TPU:26, one launch (start us, length us, event | category | flops | bytes accessed | tf_op | source)
XLA Modules:
  0.0 20.5 jit_solution(3931682643329537496)
XLA Ops:
  0.0 0.0 collective-permute-start.1
  0.0 1.6 %collective-permute-start = (f32[2,96,128]{2,1,0:T(8,128)}, f32[2,96,128]{2,1,0:T(8,128)S(1)}, u32[]{:S(2)}, u32[]{:S(2)}) collective-permute-start(f32[2,96,128]{2,1,0:T(8,128)} %bitcast.17), channel_id=1, source_target_pairs={{0,1},{1,0},{2,3},{3,2},{4,5},{5,4},{6,7},{7,6},{8,9},{9,8},{10,11... | collective-permute-start | bytes 294920 | tf_op jit(solution)/shard_map/ppermute | solution.py:555
  1.6 1.7 %load.1 = (f32[48,1024]{1,0:T(8,128)S(1)}, f32[48,1024]{1,0:T(8,128)S(1)}, bf16[32,1024]{1,0:T(8,128)(2,1)S(1)}, bf16[1024,1024]{1,0:T(8,128)(2,1)S(1)}, bf16[16...) custom-call(s32[8]{0:T(128)} %bitcast.15, ...), custom_call_target="tpu_custom_call" | custom-call | tf_op jit(solution)/shard_map/load/pallas_call | solution.py:560
  3.3 1.7 %products.1 = (f32[96,1024]{1,0:T(8,128)S(1)}, f32[16,1024]{1,0:T(8,128)S(1)}, bf16[1920,256]{1,0:T(8,128)(2,1)S(1)}) custom-call(f32[48,1024]{1,0:T(8,128)S(1)} %get-tuple-element.49.ti, bf16[32,1024]{1,0:T(8,128)(2,1)S(1)} %get-tuple-element.50.mix, bf16[16,32,1024]{2,1,0:T(8,128)(2,1)S(1)} %get-tuple-element.48.rhs.refs_8_.refs_11_, ...), custom_call_target="tpu_custom_call" | custom-call | tf_op jit(solution)/shard_map/products/pallas_call | solution.py:608
  5.0 0.0 collective-permute-done.1.ring_b
  5.0 0.0 collective-permute-done.ring_a
  5.0 1.0 %collective-permute-start.2 = (f32[96,128]{1,0:T(8,128)S(1)}, f32[96,128]{1,0:T(8,128)S(1)}, u32[]{:S(2)}, u32[]{:S(2)}) collective-permute-start(f32[96,128]{1,0:T(8,128)S(1)} %get-tuple-element.57), channel_id=1, source_target_pairs={{0,8},{1,9},{2,10},{3,11},{4,12},{5,13},{6,14},{7,15},{8,0},{9,1},... | collective-permute-start | bytes 147464 | tf_op jit(solution)/shard_map/ppermute | solution.py:652
  6.0 1.8 %rim_rest.1 = (f32[96,1024]{1,0:T(8,128)S(1)}, bf16[128,2048]{1,0:T(8,128)(2,1)S(1)}, bf16[1024,1024]{1,0:T(8,128)(2,1)S(1)}, f32[1,1024]{1,0:T(1,128)S(1)}) custom-call(f32[2,96,128]{2,1,0:T(8,128)S(1)} %collective-permute-done.ring_a, f32[2,96,128]{2,1,0:T(8,128)S(1)} %collective-permute-done.1.ring_b, ...), custom_call_target="tpu_custom_call", output_to_operand_aliasing={{0}: (6, {})} | custom-call | tf_op jit(solution)/shard_map/rim_rest/pallas_call | solution.py:654
  7.8 0.0 collective-permute-done.2.refs_0_
  7.9 1.4 %turn1.1 = (f32[16,32,1024]{2,1,0:T(8,128)S(1)}, bf16[192,1024]{1,0:T(8,128)(2,1)S(1)}, f32[96,128]{1,0:T(8,128)S(1)}) custom-call(f32[96,128]{1,0:T(8,128)S(1)} %collective-permute-done.2.refs_0_, f32[1,1024]{1,0:T(1,128)S(1)} %get-tuple-element.41.live.refs_0_.refs_1_, ...), custom_call_target="tpu_custom_call", output_to_operand_aliasing={{0}: (12, {}), {1}: (13, {})} | custom-call | tf_op jit(solution)/shard_map/turn1/pallas_call | solution.py:638
  9.3 0.1 collective-permute-start.3
  9.4 1.2 %collective-permute-done.3.refs_0_ = f32[96,128]{1,0:T(8,128)S(1)} collective-permute-done((f32[96,128]{1,0:T(8,128)S(1)}, f32[96,128]{1,0:T(8,128)S(1)}, u32[]{:S(2)}, u32[]{:S(2)}) %collective-permute-start.3) | collective-permute-done | bytes 49184 | tf_op jit(solution)/shard_map/ppermute | solution.py:652
  10.6 1.4 %turn2.1 = (f32[16,32,1024]{2,1,0:T(8,128)S(1)}, bf16[192,1024]{1,0:T(8,128)(2,1)S(1)}, f32[96,128]{1,0:T(8,128)S(1)}) custom-call(f32[96,128]{1,0:T(8,128)S(1)} %collective-permute-done.3.refs_0_, f32[1,1024]{1,0:T(1,128)S(1)} %get-tuple-element.41.live.refs_0_.refs_1_, ...), custom_call_target="tpu_custom_call", output_to_operand_aliasing={{0}: (12, {}), {1}: (13, {})} | custom-call | tf_op jit(solution)/shard_map/turn2/pallas_call | solution.py:638
  12.0 3.0 %collective-permute-start.4 = (f32[96,128]{1,0:T(8,128)S(1)}, f32[96,128]{1,0:T(8,128)S(1)}, u32[]{:S(2)}, u32[]{:S(2)}) collective-permute-start(f32[96,128]{1,0:T(8,128)S(1)} %get-tuple-element.65), channel_id=1, source_target_pairs={{0,1},{1,0},{2,3},{3,2},{4,5},{5,4},{6,7},{7,6},{8,9},{9,8},{10,11... | collective-permute-start | bytes 147464 | tf_op jit(solution)/shard_map/ppermute | solution.py:652
  15.0 2.0 %collective-permute-done.4.refs_0_ = f32[96,128]{1,0:T(8,128)S(1)} collective-permute-done((f32[96,128]{1,0:T(8,128)S(1)}, f32[96,128]{1,0:T(8,128)S(1)}, u32[]{:S(2)}, u32[]{:S(2)}) %collective-permute-start.4) | collective-permute-done | bytes 49184 | tf_op jit(solution)/shard_map/ppermute | solution.py:652
  17.1 1.2 %turn3.1 = (f32[16,32,1024]{2,1,0:T(8,128)S(1)}, bf16[192,1024]{1,0:T(8,128)(2,1)S(1)}) custom-call(f32[96,128]{1,0:T(8,128)S(1)} %collective-permute-done.4.refs_0_, f32[1,1024]{1,0:T(1,128)S(1)} %get-tuple-element.41.live.refs_0_.refs_1_, f32[96,1024]{1,0:T(8,128)S(1)} %get-tuple-element.52.refs_1_.refs_2_, ...), custom_call_target="tpu_custom_call", output_to_operand_aliasing={{0}: (12, {}), {1}: (13, {})} | custom-call | tf_op jit(solution)/shard_map/turn3/pallas_call | solution.py:638
  18.2 2.3 %final.1 = (f32[16,32,1024]{2,1,0:T(8,128)S(1)}, f32[16,32,1024]{2,1,0:T(8,128)}) custom-call(f32[1,1024]{1,0:T(1,128)S(1)} %get-tuple-element.46.mask.refs_9_, bf16[16,16,1024]{2,1,0:T(8,128)(2,1)S(1)} %get-tuple-element.47.refs_7_.refs_10_.inv, ...), custom_call_target="tpu_custom_call", output_to_operand_aliasing={{0}: (6, {}), {1}: (7, {})} | custom-call | tf_op jit(solution)/shard_map/final/pallas_call | solution.py:707
  (5 shorter events, 0.1 us)
Async XLA Ops:
  0.0 5.0 %collective-permute-start.1 = (f32[2,96,128]{2,1,0:T(8,128)}, f32[2,96,128]{2,1,0:T(8,128)S(1)}, u32[]{:S(2)}, u32[]{:S(2)}) collective-permute-start(f32[2,96,128]{2,1,0:T(8,128)} %bitcast.16), channel_id=1, source_target_pairs={{0,8},{1,2},{2,1},{3,4},{4,3},{5,6},{6,5},{7,15},{8,0},{9,10},{10,... | collective-permute-start | bytes 294920 | tf_op jit(solution)/shard_map/ppermute | solution.py:556
  0.0 5.0 %collective-permute-start = (f32[2,96,128]{2,1,0:T(8,128)}, f32[2,96,128]{2,1,0:T(8,128)S(1)}, u32[]{:S(2)}, u32[]{:S(2)}) collective-permute-start(f32[2,96,128]{2,1,0:T(8,128)} %bitcast.17), channel_id=1, source_target_pairs={{0,1},{1,0},{2,3},{3,2},{4,5},{5,4},{6,7},{7,6},{8,9},{9,8},{10,11... | collective-permute-start | bytes 294920 | tf_op jit(solution)/shard_map/ppermute | solution.py:555
  5.0 2.8 %collective-permute-start.2 = (f32[96,128]{1,0:T(8,128)S(1)}, f32[96,128]{1,0:T(8,128)S(1)}, u32[]{:S(2)}, u32[]{:S(2)}) collective-permute-start(f32[96,128]{1,0:T(8,128)S(1)} %get-tuple-element.57), channel_id=1, source_target_pairs={{0,8},{1,9},{2,10},{3,11},{4,12},{5,13},{6,14},{7,15},{8,0},{9,1},... | collective-permute-start | bytes 147464 | tf_op jit(solution)/shard_map/ppermute | solution.py:652
  9.3 1.3 %collective-permute-start.3 = (f32[96,128]{1,0:T(8,128)S(1)}, f32[96,128]{1,0:T(8,128)S(1)}, u32[]{:S(2)}, u32[]{:S(2)}) collective-permute-start(f32[96,128]{1,0:T(8,128)S(1)} %get-tuple-element.62), channel_id=1, source_target_pairs={{0,1},{1,0},{2,3},{3,2},{4,5},{5,4},{6,7},{7,6},{8,16},{9,17},{10,... | collective-permute-start | bytes 147464 | tf_op jit(solution)/shard_map/ppermute | solution.py:652
  12.0 5.1 %collective-permute-start.4 = (f32[96,128]{1,0:T(8,128)S(1)}, f32[96,128]{1,0:T(8,128)S(1)}, u32[]{:S(2)}, u32[]{:S(2)}) collective-permute-start(f32[96,128]{1,0:T(8,128)S(1)} %get-tuple-element.65), channel_id=1, source_target_pairs={{0,1},{1,0},{2,3},{3,2},{4,5},{5,4},{6,7},{7,6},{8,9},{9,8},{10,11... | collective-permute-start | bytes 147464 | tf_op jit(solution)/shard_map/ppermute | solution.py:652

commit v5 on v4

--- a/solution.py
+++ b/solution.py
@@ -145,12 +145,11 @@
             high, low = split(sums[f])
             stacked[f * tracers : (f + 1) * tracers, at] = high
             stacked[half + f * tracers : half + (f + 1) * tracers, at] = low
+        own_weights(j, index, weights, own)
         if (j + 1) % (groups // 4) == 0:
             part = pl.ds((j + 1 - groups // 4) * LANES, groups // 4 * LANES)
             term = jnp.dot(stacked[:, part], q[part, :], preferred_element_type=F32)
             slots = term if slots is None else slots + term
-    for level in range(groups):
-        own_weights(level, index, weights, own)
     slots = slots[:half] + slots[half:]
     r_out[...] = slots[:rows] * live[...]
     w_out[...] = slots[rows:] * live[...]

time: 20.8 us -> 20.8 us (level)
  no operation moved by 1% of the time
where the time goes in v5:
time: 20.8 us; the launch traced here: 20.6 us
  Pallas kernels  11.5 us (55%)
  starting transfers between devices  5.74 us (28%)
  waiting for transfers between devices  3.2 us (15%)
    ppermute x3, starting transfers between devices, shards(): lax.ppermute(made[2], axes, swaps(flows, columns, hop_partner(moment)))  4.14 us
    pallas_call x4, Pallas kernels, shards(): pl.pallas_call(functools.partial(turn, moment=moment, flow='flow', face_d...  3.95 us
    ppermute x3, waiting for transfers between devices, shards(): lax.ppermute(made[2], axes, swaps(flows, columns, hop_partner(moment)))  3.19 us
    pallas_call x1, Pallas kernels, shards(): pl.pallas_call(functools.partial(final, flow='flow'), out_shape=[p_shape,...  2.28 us
    pallas_call x1, Pallas kernels, shards(): pl.pallas_call(functools.partial(rim_rest, axes=axes), out_shape=[e_shape...  1.84 us
    pallas_call x1, Pallas kernels, shards(): pl.pallas_call(products, out_shape=[pltpu.VMEM((rows, cells), F32), pltpu...  1.7 us
    pallas_call x1, Pallas kernels, shards(): pl.pallas_call(load, out_shape=(pltpu.VMEM((face_dofs * block, cells), F3...  1.69 us
    ppermute x1, starting transfers between devices, shards(): lax.ppermute(edges, axes, swaps(flows, columns, rim_partner(0, columns)))  1.6 us
  transfers between devices with their start and end apart: 5, of which 2 were waited for; matrix products, arithmetic and copies ran while one was open for 0% of the time, Pallas kernels for 26%

profile of v5, /device:TPU:26, one launch (start us, length us, event | category | flops | bytes accessed | tf_op | source)
XLA Modules:
  0.0 20.6 jit_solution(16713292864091348979)
XLA Ops:
  0.0 0.0 collective-permute-start.1
  0.0 1.6 %collective-permute-start = (f32[2,96,128]{2,1,0:T(8,128)}, f32[2,96,128]{2,1,0:T(8,128)S(1)}, u32[]{:S(2)}, u32[]{:S(2)}) collective-permute-start(f32[2,96,128]{2,1,0:T(8,128)} %bitcast.17), channel_id=1, source_target_pairs={{0,1},{1,0},{2,3},{3,2},{4,5},{5,4},{6,7},{7,6},{8,9},{9,8},{10,11... | collective-permute-start | bytes 294920 | tf_op jit(solution)/shard_map/ppermute | solution.py:554
  1.6 1.7 %load.1 = (f32[48,1024]{1,0:T(8,128)S(1)}, f32[48,1024]{1,0:T(8,128)S(1)}, bf16[32,1024]{1,0:T(8,128)(2,1)S(1)}, bf16[1024,1024]{1,0:T(8,128)(2,1)S(1)}, bf16[16...) custom-call(s32[8]{0:T(128)} %bitcast.15, ...), custom_call_target="tpu_custom_call" | custom-call | tf_op jit(solution)/shard_map/load/pallas_call | solution.py:559
  3.3 1.7 %products.1 = (f32[96,1024]{1,0:T(8,128)S(1)}, f32[16,1024]{1,0:T(8,128)S(1)}, bf16[1920,256]{1,0:T(8,128)(2,1)S(1)}) custom-call(f32[48,1024]{1,0:T(8,128)S(1)} %get-tuple-element.49.ti, bf16[32,1024]{1,0:T(8,128)(2,1)S(1)} %get-tuple-element.50.mix, bf16[16,32,1024]{2,1,0:T(8,128)(2,1)S(1)} %get-tuple-element.48.rhs.refs_8_.refs_11_, ...), custom_call_target="tpu_custom_call" | custom-call | tf_op jit(solution)/shard_map/products/pallas_call | solution.py:607
  5.0 0.0 collective-permute-done.1.ring_b
  5.0 0.0 collective-permute-done.ring_a
  5.1 0.9 %collective-permute-start.2 = (f32[96,128]{1,0:T(8,128)S(1)}, f32[96,128]{1,0:T(8,128)S(1)}, u32[]{:S(2)}, u32[]{:S(2)}) collective-permute-start(f32[96,128]{1,0:T(8,128)S(1)} %get-tuple-element.57), channel_id=1, source_target_pairs={{0,8},{1,9},{2,10},{3,11},{4,12},{5,13},{6,14},{7,15},{8,0},{9,1},... | collective-permute-start | bytes 147464 | tf_op jit(solution)/shard_map/ppermute | solution.py:651
  6.0 1.8 %rim_rest.1 = (f32[96,1024]{1,0:T(8,128)S(1)}, bf16[128,2048]{1,0:T(8,128)(2,1)S(1)}, bf16[1024,1024]{1,0:T(8,128)(2,1)S(1)}, f32[1,1024]{1,0:T(1,128)S(1)}) custom-call(f32[2,96,128]{2,1,0:T(8,128)S(1)} %collective-permute-done.ring_a, f32[2,96,128]{2,1,0:T(8,128)S(1)} %collective-permute-done.1.ring_b, ...), custom_call_target="tpu_custom_call", output_to_operand_aliasing={{0}: (6, {})} | custom-call | tf_op jit(solution)/shard_map/rim_rest/pallas_call | solution.py:653
  7.8 0.0 collective-permute-done.2.refs_0_
  7.9 1.4 %turn1.1 = (f32[16,32,1024]{2,1,0:T(8,128)S(1)}, bf16[192,1024]{1,0:T(8,128)(2,1)S(1)}, f32[96,128]{1,0:T(8,128)S(1)}) custom-call(f32[96,128]{1,0:T(8,128)S(1)} %collective-permute-done.2.refs_0_, f32[1,1024]{1,0:T(1,128)S(1)} %get-tuple-element.41.live.refs_0_.refs_1_, ...), custom_call_target="tpu_custom_call", output_to_operand_aliasing={{0}: (12, {}), {1}: (13, {})} | custom-call | tf_op jit(solution)/shard_map/turn1/pallas_call | solution.py:637
  9.3 0.1 collective-permute-start.3
  9.4 1.2 %collective-permute-done.3.refs_0_ = f32[96,128]{1,0:T(8,128)S(1)} collective-permute-done((f32[96,128]{1,0:T(8,128)S(1)}, f32[96,128]{1,0:T(8,128)S(1)}, u32[]{:S(2)}, u32[]{:S(2)}) %collective-permute-start.3) | collective-permute-done | bytes 49184 | tf_op jit(solution)/shard_map/ppermute | solution.py:651
  10.6 1.4 %turn2.1 = (f32[16,32,1024]{2,1,0:T(8,128)S(1)}, bf16[192,1024]{1,0:T(8,128)(2,1)S(1)}, f32[96,128]{1,0:T(8,128)S(1)}) custom-call(f32[96,128]{1,0:T(8,128)S(1)} %collective-permute-done.3.refs_0_, f32[1,1024]{1,0:T(1,128)S(1)} %get-tuple-element.41.live.refs_0_.refs_1_, ...), custom_call_target="tpu_custom_call", output_to_operand_aliasing={{0}: (12, {}), {1}: (13, {})} | custom-call | tf_op jit(solution)/shard_map/turn2/pallas_call | solution.py:637
  12.0 3.1 %collective-permute-start.4 = (f32[96,128]{1,0:T(8,128)S(1)}, f32[96,128]{1,0:T(8,128)S(1)}, u32[]{:S(2)}, u32[]{:S(2)}) collective-permute-start(f32[96,128]{1,0:T(8,128)S(1)} %get-tuple-element.65), channel_id=1, source_target_pairs={{0,1},{1,0},{2,3},{3,2},{4,5},{5,4},{6,7},{7,6},{8,9},{9,8},{10,11... | collective-permute-start | bytes 147464 | tf_op jit(solution)/shard_map/ppermute | solution.py:651
  15.1 2.0 %collective-permute-done.4.refs_0_ = f32[96,128]{1,0:T(8,128)S(1)} collective-permute-done((f32[96,128]{1,0:T(8,128)S(1)}, f32[96,128]{1,0:T(8,128)S(1)}, u32[]{:S(2)}, u32[]{:S(2)}) %collective-permute-start.4) | collective-permute-done | bytes 49184 | tf_op jit(solution)/shard_map/ppermute | solution.py:651
  17.2 1.2 %turn3.1 = (f32[16,32,1024]{2,1,0:T(8,128)S(1)}, bf16[192,1024]{1,0:T(8,128)(2,1)S(1)}) custom-call(f32[96,128]{1,0:T(8,128)S(1)} %collective-permute-done.4.refs_0_, f32[1,1024]{1,0:T(1,128)S(1)} %get-tuple-element.41.live.refs_0_.refs_1_, f32[96,1024]{1,0:T(8,128)S(1)} %get-tuple-element.52.refs_1_.refs_2_, ...), custom_call_target="tpu_custom_call", output_to_operand_aliasing={{0}: (12, {}), {1}: (13, {})} | custom-call | tf_op jit(solution)/shard_map/turn3/pallas_call | solution.py:637
  18.3 2.3 %final.1 = (f32[16,32,1024]{2,1,0:T(8,128)S(1)}, f32[16,32,1024]{2,1,0:T(8,128)}) custom-call(f32[1,1024]{1,0:T(1,128)S(1)} %get-tuple-element.46.mask.refs_9_, bf16[16,16,1024]{2,1,0:T(8,128)(2,1)S(1)} %get-tuple-element.47.refs_7_.refs_10_.inv, ...), custom_call_target="tpu_custom_call", output_to_operand_aliasing={{0}: (6, {}), {1}: (7, {})} | custom-call | tf_op jit(solution)/shard_map/final/pallas_call | solution.py:706
  (5 shorter events, 0.1 us)
Async XLA Ops:
  0.0 5.0 %collective-permute-start.1 = (f32[2,96,128]{2,1,0:T(8,128)}, f32[2,96,128]{2,1,0:T(8,128)S(1)}, u32[]{:S(2)}, u32[]{:S(2)}) collective-permute-start(f32[2,96,128]{2,1,0:T(8,128)} %bitcast.16), channel_id=1, source_target_pairs={{0,8},{1,2},{2,1},{3,4},{4,3},{5,6},{6,5},{7,15},{8,0},{9,10},{10,... | collective-permute-start | bytes 294920 | tf_op jit(solution)/shard_map/ppermute | solution.py:555
  0.0 5.0 %collective-permute-start = (f32[2,96,128]{2,1,0:T(8,128)}, f32[2,96,128]{2,1,0:T(8,128)S(1)}, u32[]{:S(2)}, u32[]{:S(2)}) collective-permute-start(f32[2,96,128]{2,1,0:T(8,128)} %bitcast.17), channel_id=1, source_target_pairs={{0,1},{1,0},{2,3},{3,2},{4,5},{5,4},{6,7},{7,6},{8,9},{9,8},{10,11... | collective-permute-start | bytes 294920 | tf_op jit(solution)/shard_map/ppermute | solution.py:554
  5.1 2.8 %collective-permute-start.2 = (f32[96,128]{1,0:T(8,128)S(1)}, f32[96,128]{1,0:T(8,128)S(1)}, u32[]{:S(2)}, u32[]{:S(2)}) collective-permute-start(f32[96,128]{1,0:T(8,128)S(1)} %get-tuple-element.57), channel_id=1, source_target_pairs={{0,8},{1,9},{2,10},{3,11},{4,12},{5,13},{6,14},{7,15},{8,0},{9,1},... | collective-permute-start | bytes 147464 | tf_op jit(solution)/shard_map/ppermute | solution.py:651
  9.3 1.3 %collective-permute-start.3 = (f32[96,128]{1,0:T(8,128)S(1)}, f32[96,128]{1,0:T(8,128)S(1)}, u32[]{:S(2)}, u32[]{:S(2)}) collective-permute-start(f32[96,128]{1,0:T(8,128)S(1)} %get-tuple-element.62), channel_id=1, source_target_pairs={{0,1},{1,0},{2,3},{3,2},{4,5},{5,4},{6,7},{7,6},{8,16},{9,17},{10,... | collective-permute-start | bytes 147464 | tf_op jit(solution)/shard_map/ppermute | solution.py:651
  12.0 5.2 %collective-permute-start.4 = (f32[96,128]{1,0:T(8,128)S(1)}, f32[96,128]{1,0:T(8,128)S(1)}, u32[]{:S(2)}, u32[]{:S(2)}) collective-permute-start(f32[96,128]{1,0:T(8,128)S(1)} %get-tuple-element.65), channel_id=1, source_target_pairs={{0,1},{1,0},{2,3},{3,2},{4,5},{5,4},{6,7},{7,6},{8,9},{9,8},{10,11... | collective-permute-start | bytes 147464 | tf_op jit(solution)/shard_map/ppermute | solution.py:651
